TPU v7x, 32 devices: a whole 2x2x4 slice. The times are simulated.
32 devices in a mesh: replica: 8 (over y, x, core), tok: 4 (over z).
Axes of the slice: x: 2, y: 2, z: 4, core: 2. Of those that a mesh axis runs over, the one named last changes fastest.
Arguments:
- activations: bfloat16 [8192, 2880], P(('replica', 'tok')), may hold values from -6 to 6
- cotangent: bfloat16 [8192, 512], P(('replica', 'tok')), may hold values from -6 to 6
- next_inputs: bfloat16 [8192, 2880], P(('replica', 'tok')), may hold values from -6 to 6
- weight_tiles: bfloat16 [360, 4096], P('tok'), may hold values from -0.109375 to 0.109375
- momentum: float32 [8, 360, 4096], P('replica', 'tok'), may hold values from -6 to 6
- chosen: int32 [8, 4, 8], P('replica', 'tok'), may hold values from 0 to 89, as said below
- counts: int32 [8, 4], P('replica', 'tok'), may hold values from 1 to 8, as said below
Outputs:
- values: bfloat16 [8192, 512], P(('replica', 'tok'))
- new_momentum: float32 [8, 360, 4096], P('replica', 'tok')
Inputs may be any that keep to these rules, and one draw needn't show every extreme that they name: Each list chosen[r, k] names 8 different tile numbers of the shard's 90 tiles; only the first counts[r, k] of them are selected. `counts`: in every draw some token shard has 8 selected tiles in every replica.
All inputs are finite; a program needn't handle non-finite values.
Results may differ from a plain program's by a relative error of at most 0.015.
Values may be sent and summed in bfloat16 or wider, within the bound.
No kernel may reach another device: no remote copies, remote signals or barrier semaphores. Data moves between devices by JAX's collectives and lax.ppermute only.
A program may use at most 64 MiB of HBM per device.

v0:
```python
import functools
import math

import jax
import jax.numpy as jnp
import numpy as np
from jax import lax
from jax.experimental import pallas as pl
from jax.experimental.pallas import tpu as pltpu
from jax.sharding import PartitionSpec as P


TILE = 64
KEEP = 32
LANES = 128


momentum_decay = 0.9
step_size = 0.01

HIGHEST = lax.Precision.HIGHEST

TOK_ORDER = (0, 2, 1, 3)
SHARE_ORDER = (0, 2, 4, 1, 3, 5, 6, 7)
HELD_ORDER = (0, 2, 4, 6, 6, 1, 3, 5, 7, 7)


def cosine_rows(count):
    frequency = jnp.arange(count, dtype=jnp.float32)[:, None]
    position = jnp.arange(TILE, dtype=jnp.float32)[None, :]
    cosines = jnp.cos(math.pi * (2.0 * position + 1.0) * frequency / (2.0 * TILE))
    factor = jnp.where(frequency == 0, math.sqrt(1.0 / TILE), math.sqrt(2.0 / TILE))
    return cosines * factor


def rebuild(summed, weight_part, keep_rows):
    quads = summed.reshape(summed.shape[0], KEEP, KEEP)
    update = jnp.einsum("ua,tuv,vb->tab", keep_rows, quads, keep_rows, precision=HIGHEST)
    shifted = weight_part.astype(jnp.float32) - step_size * update.reshape(
        summed.shape[0], TILE * TILE
    )
    return shifted.astype(jnp.bfloat16)


def forward(inputs, new_tiles):
    row_tiles = inputs.shape[1] // TILE
    col_tiles = new_tiles.shape[0] // row_tiles
    blocks = inputs.reshape(inputs.shape[0], row_tiles, TILE)
    matrix = new_tiles.reshape(row_tiles, col_tiles, TILE, TILE)
    output = jnp.einsum("tra,rcab->tcb", blocks, matrix, preferred_element_type=jnp.float32)
    return output.reshape(inputs.shape[0], col_tiles * TILE).astype(jnp.bfloat16)


def general(activations, cotangent, next_inputs, weight_tiles, momentum, chosen, counts):
    shards = lax.axis_size("tok")
    tiles_here = weight_tiles.shape[0]
    row_tiles = activations.shape[1] // TILE
    col_tiles = cotangent.shape[1] // TILE
    grad_scale = 1.0 / math.sqrt(activations.shape[0] * shards)
    keep_rows = cosine_rows(KEEP)
    product = (
        lax.dot_general(
            activations, cotangent, (((0,), (0,)), ((), ())), preferred_element_type=jnp.float32
        )
        * grad_scale
    )
    tiled = product.reshape(row_tiles, TILE, col_tiles, TILE).transpose(0, 2, 1, 3)
    tiled = tiled.reshape(row_tiles * col_tiles, TILE * TILE)
    gradient = lax.psum_scatter(
        tiled.astype(jnp.bfloat16), "tok", scatter_dimension=0, tiled=True
    ).astype(jnp.float32)
    updated = momentum_decay * momentum[0] + gradient
    chosen_here = chosen[0, 0]
    in_list = jnp.arange(chosen_here.shape[0], dtype=jnp.int32) < counts[0, 0]
    picked = jnp.take(updated, chosen_here, axis=0).reshape(-1, TILE, TILE)
    quadrant = jnp.einsum("ua,nab,vb->nuv", keep_rows, picked, keep_rows, precision=HIGHEST)
    quadrant = jnp.where(in_list[:, None, None], quadrant, 0.0).astype(jnp.bfloat16)
    rebuilt = jnp.einsum(
        "ua,nuv,vb->nab", keep_rows, quadrant.astype(jnp.float32), keep_rows, precision=HIGHEST
    )
    new_momentum = updated.at[chosen_here].add(-rebuilt.reshape(-1, TILE * TILE))
    listed = jnp.where(in_list, chosen_here, -1)
    flat_quads = quadrant.reshape(-1, KEEP * KEEP)
    tile_numbers = jnp.arange(tiles_here, dtype=jnp.int32)
    all_quads, all_listed = (
        lax.all_gather(flat_quads, "replica", axis=0, tiled=True),
        lax.all_gather(listed, "replica", axis=0, tiled=True),
    )
    one_hot = (all_listed[:, None] == tile_numbers[None, :]).astype(jnp.bfloat16)
    summed = lax.dot_general(
        one_hot, all_quads, (((0,), (0,)), ((), ())), preferred_element_type=jnp.float32
    )
    new_part = rebuild(summed, weight_tiles, keep_rows)
    new_full = lax.all_gather(new_part, "tok", axis=0, tiled=True)
    values = forward(next_inputs, new_full)
    return (values, new_momentum[None])


def low_rows():
    u = np.arange(KEEP)[:, None].astype(np.float64)
    i = np.arange(TILE)[None, :].astype(np.float64)
    factor = np.where(u == 0, math.sqrt(1.0 / TILE), math.sqrt(2.0 / TILE))
    return np.cos(math.pi * (2 * i + 1) * u / (2 * TILE)) * factor


def tables():
    low = low_rows()
    split = np.concatenate([low[:, 0::2], low[:, 1::2]], axis=0)
    into = np.zeros((4 * LANES, LANES))
    back = np.zeros((LANES, 4 * LANES))
    for g in range(4):
        into[g * LANES : g * LANES + TILE, g * KEEP : (g + 1) * KEEP] = low.T
        for half in range(2):
            at = g * LANES + half * TILE
            back[g * KEEP : (g + 1) * KEEP, at : at + TILE] = low
    split_back = np.concatenate([low[:, 0::2].T, low[:, 1::2].T], axis=0)
    return [t.astype(np.float32) for t in (split, into, split_back, back)]


def lane_index(shape):
    return lax.broadcasted_iota(jnp.int32, shape, len(shape) - 1)


def tile_products(act_ref, cot_ref, sent_ref, cot_row, grid_ref, tiled_ref, scale, spans):
    tokens = act_ref.shape[1]
    width = cot_ref.shape[1]
    first_half = lane_index((KEEP, LANES)) < TILE
    step = 2 * TILE
    theirs = [
        sent_ref[0][cot_row + n * tokens : cot_row + (n + 1) * tokens, :]
        for n in range(width // tokens)
    ]
    for block in range(spans // 2):
        rows = slice(block * step, (block + 1) * step)
        mine = jnp.dot(act_ref[rows, :], cot_ref[...], preferred_element_type=jnp.float32)
        other = sent_ref[1][rows, :]
        for n, piece in enumerate(theirs):
            lanes = slice(n * tokens, (n + 1) * tokens)
            theirs_here = jnp.dot(other, piece, preferred_element_type=jnp.float32)
            both = (mine[:, lanes] + theirs_here) * scale
            for m in range(tokens // LANES):
                grid_ref[n * (tokens // LANES) + m] = both[:, m * LANES : (m + 1) * LANES]
        for half in range(2):
            for m in range(width // LANES):
                even = grid_ref[m, pl.ds(half * TILE, KEEP, stride=2), :]
                odd = grid_ref[m, pl.ds(half * TILE + 1, KEEP, stride=2), :]
                tile = (2 * block + half) * (width // TILE) + 2 * m
                tiled_ref[tile * KEEP : (tile + 1) * KEEP, :] = jnp.where(
                    first_half, even, pltpu.roll(odd, TILE, 1)
                )
                tiled_ref[(tile + 1) * KEEP : (tile + 2) * KEEP, :] = jnp.where(
                    first_half, pltpu.roll(even, TILE, 1), odd
                )


def to_low(picked, split_ref, into_ref):
    wide = jnp.concatenate(picked, axis=1)
    mixed = jnp.dot(split_ref[...], wide, preferred_element_type=jnp.float32)
    out = []
    for h in range(len(picked) // 4):
        pieces = []
        for g in range(4):
            lanes = slice((4 * h + g) * LANES, (4 * h + g + 1) * LANES)
            pieces.append(mixed[:KEEP, lanes] + pltpu.roll(mixed[KEEP:, lanes], TILE, 1))
        row = jnp.concatenate(pieces, axis=1)
        out.append(jnp.dot(row, into_ref[...], preferred_element_type=jnp.float32))
    return out


def far_kernel(
    chosen_ref, act_ref, cot_ref, sent_ref, split_ref, into_ref,
    low_ref, *rest, scale, spans, tiles_here,
):
    sum_refs, (grid_ref, tiled_ref) = rest[:-2], rest[-2:]
    skip = first_skip(lax.axis_index("tok") ^ 2, tiles_here, cot_ref.shape[1] // TILE)
    tile_products(
        act_ref, cot_ref, (sent_ref, sent_ref), spans * TILE, grid_ref, tiled_ref, scale, spans
    )
    slots = chosen_ref.shape[0]
    picked = [
        tiled_ref[pl.ds(pl.multiple_of((skip + chosen_ref[s]) * KEEP, KEEP), KEEP), :]
        for s in range(slots)
    ]
    for h, part in enumerate(to_low(picked, split_ref, into_ref)):
        low_ref[h * KEEP : (h + 1) * KEEP, :] = part
    first = 0
    for sum_ref in sum_refs:
        rows = sum_ref.shape[0]
        for c in range(0, rows, 2 * KEEP):
            n = min(2 * KEEP, rows - c)
            sum_ref[c : c + n, :] = tiled_ref[
                pl.ds(pl.multiple_of(skip * KEEP + first + c, KEEP), n), :
            ].astype(jnp.bfloat16)
        first += rows


def own_kernel(
    count_ref, chosen_ref, act_ref, cot_ref, sent_ref, near_ref, mom_ref, far_low_ref,
    split_ref, into_ref, split_back_ref, back_ref,
    part_ref, quad_ref, grid_ref, tiled_ref, held_ref, sems, *, scale, spans, tiles_here,
):
    skip = first_skip(lax.axis_index("tok"), tiles_here, cot_ref.shape[1] // TILE)
    count = count_ref[0]
    slots = chosen_ref.shape[0]
    copies = [
        pltpu.make_async_copy(
            mom_ref.at[pl.ds(pl.multiple_of(chosen_ref[s] * KEEP, KEEP), KEEP)],
            held_ref.at[s], sems.at[s],
        )
        for s in range(slots)
    ]
    for copy in copies:
        copy.start()
    tile_products(
        act_ref, cot_ref, (sent_ref, near_ref), spans * TILE, grid_ref, tiled_ref, scale, spans
    )
    for copy in copies:
        copy.wait()
    places = [
        pl.ds(pl.multiple_of((skip + chosen_ref[s]) * KEEP, KEEP), KEEP) for s in range(slots)
    ]
    picked = [momentum_decay * held_ref[s] + tiled_ref[places[s], :] for s in range(slots)]
    lows = to_low(picked, split_ref, into_ref)
    group = lane_index((KEEP, LANES)) // KEEP
    first_half = lax.rem(lane_index((KEEP, 4 * LANES)), LANES) < TILE
    for h, low in enumerate(lows):
        low = low + far_low_ref[h * KEEP : (h + 1) * KEEP, :]
        quad = jnp.where(group + 4 * h < count, low, 0.0).astype(jnp.bfloat16)
        quad_ref[h * KEEP : (h + 1) * KEEP, :] = quad
        wide = jnp.dot(
            quad.astype(jnp.float32), back_ref[...], preferred_element_type=jnp.float32
        )
        both = jnp.dot(split_back_ref[...], wide, preferred_element_type=jnp.float32)
        rebuilt = jnp.where(first_half, both[:KEEP, :], both[KEEP:, :])
        for g in range(4):
            place = places[4 * h + g]
            tiled_ref[place, :] = tiled_ref[place, :] - rebuilt[:, g * LANES : (g + 1) * LANES]
    rows = part_ref.shape[0]
    for c in range(0, rows, 2 * KEEP):
        part_ref[c : c + 2 * KEEP, :] = tiled_ref[
            pl.ds(pl.multiple_of(skip * KEEP + c, KEEP), 2 * KEEP), :
        ].astype(jnp.bfloat16)


def first_row(shard, tiles_here, col_tiles):
    return pl.multiple_of((shard * tiles_here) // col_tiles * TILE, TILE)


def first_skip(shard, tiles_here, col_tiles):
    return lax.rem(shard * tiles_here, col_tiles)


def run_copies(pairs, sems):
    copies = [pltpu.make_async_copy(a, b, sems.at[n]) for n, (a, b) in enumerate(pairs)]
    for copy in copies:
        copy.start()
    for copy in copies:
        copy.wait()


def prepare_kernel(act_ref, cot_ref, far_ref, near_ref, sems, *, tiles_here):
    rows, tokens = near_ref.shape
    me = lax.axis_index("tok")
    pick = lambda n: act_ref.at[pl.ds(first_row(me ^ n, tiles_here, cot_ref.shape[1] // TILE), rows)]
    pairs = [(pick(3), far_ref.at[pl.ds(0, rows)]), (pick(1), near_ref)]
    for n in range(cot_ref.shape[1] // tokens):
        lanes, at = pl.ds(n * tokens, tokens), pl.ds(rows + n * tokens, tokens)
        pairs.append((cot_ref.at[:, lanes], far_ref.at[at]))
    run_copies(pairs, sems)


def mine_kernel(act_ref, far_ref, near_ref, sems, *, tiles_here, col_tiles):
    rows = near_ref.shape[0]
    me = lax.axis_index("tok")
    pick = lambda n: act_ref.at[pl.ds(first_row(me ^ n, tiles_here, col_tiles), rows)]
    run_copies([(pick(2), far_ref), (pick(0), near_ref)], sems)


def reorder_kernel(order_ref, from_ref, to_ref, sems):
    size = from_ref.shape[0]
    for n in range(size, to_ref.shape[1]):
        to_ref[:, n] = jnp.zeros_like(to_ref[:, n])
    run_copies(
        [
            (from_ref.at[:, order_ref[n]], to_ref.at[n, pl.ds(0, size)])
            for n in range(to_ref.shape[0])
        ],
        sems,
    )


def finish_kernel(mom_ref, part_ref, *refs):
    sums, out_ref = refs[:-1], refs[-1]
    first = 0
    for ref in sums:
        for c in range(0, ref.shape[0], 2 * KEEP):
            n = min(2 * KEEP, ref.shape[0] - c)
            rows = slice(first + c, first + c + n)
            out_ref[rows, :] = (
                momentum_decay * mom_ref[rows, :]
                + part_ref[rows, :].astype(jnp.float32)
                + ref[c : c + n, :].astype(jnp.float32)
            )
        first += ref.shape[0]


def unchanged_kernel(mine_ref, *refs, tiles_here, list_row):
    held, (out_ref, place_ref) = refs[:-2], refs[-2:]
    size = held[0].shape[0]
    me = lax.axis_index("tok")
    lane = lane_index((1, LANES))
    slots_at = [(o, [r for r, k in zip(held, HELD_ORDER) if k == o]) for o in SHARE_ORDER]
    total = None
    for n, (_, pieces) in enumerate(slots_at):
        first = n * size
        for piece in pieces:
            x = mine_ref[first : first + piece.shape[0], :]
            first += piece.shape[0]
            term = lax.dot_general(
                x, piece[...], (((0,), (0,)), ((), ())), preferred_element_type=jnp.float32
            )
            total = term if total is None else total + term
        piece = pieces[-1]
        at = list_row - (size - piece.shape[0])
        lists = piece[at : at + 8, :LANES].astype(jnp.float32).astype(jnp.int32)
        row = jnp.zeros((1, LANES), jnp.int32)
        for d, offset in enumerate(TOK_ORDER):
            tile = lists[d : d + 1, :] + (me ^ offset) * tiles_here
            i, j = lax.shift_right_logical(tile, 3), tile & 7
            packed = (lax.shift_right_logical(j, 2) * place_rows(mine_ref) + i * KEEP) * LANES
            packed = packed + (j & 3) * KEEP
            packed = pltpu.roll(packed, 8 * d, 1)
            row = jnp.where((lane >= 8 * d) & (lane < 8 * (d + 1)), packed, row)
        place_ref[n : n + 1, :] = row
    out_ref[...] = total


def place_rows(mine_ref):
    depth = mine_ref.shape[0] - 8 * len(SHARE_ORDER)
    return -(-(depth // TILE * KEEP) // LANES) * LANES


def lows_kernel(inputs_ref, high_ref, low_ref, out_ref, lows_ref, *, span):
    rows = inputs_ref.shape[0]
    half = span // 2
    lows_ref[...] = jnp.zeros_like(lows_ref)
    for c in range(rows // span):
        piece = inputs_ref[c * span : (c + 1) * span, :]
        lows_ref[c * half : (c + 1) * half, :] = jnp.dot(
            high_ref[...], piece, preferred_element_type=jnp.float32
        ) + jnp.dot(low_ref[...], piece, preferred_element_type=jnp.float32)
    out_ref[...] = lows_ref[...].T.astype(jnp.bfloat16)


def add_quads(place_ref, n, quads_ref, sum_ref):
    first_lane = lane_index((KEEP, LANES)) // KEEP * KEEP
    slots = quads_ref.shape[1] // KEEP * 4

    def add_list(d, carry):
        puts = []
        for s in range(slots):
            h, g = s // 4, s % 4
            quad = quads_ref[d, h * KEEP : (h + 1) * KEEP, :]
            packed = place_ref[n, d * slots + s]
            to = packed & (LANES - 1)
            moved = pltpu.roll(quad.astype(jnp.float32), (to - g * KEEP) & (LANES - 1), 1)
            row = pl.multiple_of(lax.shift_right_logical(packed, 7), KEEP)
            place = sum_ref.at[pl.ds(row, KEEP)]
            puts.append((place, place[...] + moved, first_lane == to))
        for place, value, mask in puts:
            pltpu.store(place, value, mask=mask)
        return carry

    lax.fori_loop(0, quads_ref.shape[0], add_list, 0)


def begin_kernel(place_ref, *refs, at):
    quads, sum_ref = refs[:-1], refs[-1]
    sum_ref[...] = jnp.zeros_like(sum_ref)
    for n, ref in zip(at, quads):
        add_quads(place_ref, n, ref, sum_ref)


def last_kernel(place_ref, lows_ref, base_ref, across_ref, begun_ref, *refs, at):
    quads, (out_ref, sum_ref) = refs[:-2], refs[-2:]
    sum_ref[...] = begun_ref[...]
    for n, ref in zip(at, quads):
        add_quads(place_ref, n, ref, sum_ref)
    rows = lows_ref.shape[1]
    whole = jnp.concatenate(
        [
            sum_ref[n * rows : (n + 1) * rows, :].astype(jnp.bfloat16)
            for n in range(sum_ref.shape[0] // rows)
        ],
        axis=1,
    )
    mixed = jnp.dot(lows_ref[...], whole, preferred_element_type=jnp.float32)
    update = jnp.dot(
        mixed.astype(jnp.bfloat16), across_ref[...], preferred_element_type=jnp.float32
    )
    out_ref[...] = (base_ref[...] - step_size * update).astype(jnp.bfloat16)


def split_bf16(table):
    top = table.astype(jnp.bfloat16)
    return top, (table - top.astype(np.float32)).astype(jnp.bfloat16)


def room(mib):
    return pltpu.CompilerParams(vmem_limit_bytes=mib * 1024 * 1024)


def vmem(count):
    return [pl.BlockSpec(memory_space=pltpu.VMEM)] * count


def smem(count):
    return [pl.BlockSpec(memory_space=pltpu.SMEM)] * count


def swap(array, axis, bit):
    size = lax.axis_size(axis)
    return lax.ppermute(array, axis, [(i, i ^ bit) for i in range(size)])


def fits(shards, replicas, activations, cotangent, weight_tiles, slots):
    tokens, depth = activations.shape
    width = cotangent.shape[1]
    tiles_here = weight_tiles.shape[0]
    span = span_of(tiles_here, width // TILE)
    return (
        shards == 4
        and replicas == 8
        and tokens % LANES == 0
        and width % tokens == 0
        and width // TILE == 8
        and slots == 8
        and depth % (5 * TILE) == 0
        and tiles_here % 10 == 0
        and tiles_here <= 256
        and slots <= 128
        and span % 2 == 0
        and all((n * tiles_here) // 8 + span <= depth // TILE for n in range(shards))
        and all((n * tiles_here) % 8 + tiles_here <= span * 8 for n in range(shards))
    )


def span_of(tiles_here, col_tiles):
    return 2 * (-(-tiles_here // col_tiles) // 2)


def local(activations, cotangent, next_inputs, weight_tiles, momentum, chosen, counts):
    shards = lax.axis_size("tok")
    replicas = lax.axis_size("replica")
    slots = chosen.shape[-1]
    if not fits(shards, replicas, activations, cotangent, weight_tiles, slots):
        return general(
            activations, cotangent, next_inputs, weight_tiles, momentum, chosen, counts
        )
    return four_shards(
        activations, cotangent, next_inputs, weight_tiles, momentum, chosen, counts
    )


def four_shards(activations, cotangent, next_inputs, weight_tiles, momentum, chosen, counts):
    shards = lax.axis_size("tok")
    replicas = lax.axis_size("replica")
    slots = chosen.shape[-1]
    tokens, depth = activations.shape
    width = cotangent.shape[1]
    tiles_here = weight_tiles.shape[0]
    row_tiles = depth // TILE
    col_tiles = width // TILE
    spans = span_of(tiles_here, col_tiles)
    span_rows = spans * TILE
    scale = 1.0 / math.sqrt(tokens * shards)
    me = lax.axis_index("tok")
    rep = lax.axis_index("replica")
    act = activations.T
    inputs = next_inputs.T
    split, into, split_back, back = tables()

    def place_of(offset):
        return (offset & 1) * 2 + lax.shift_right_logical(offset, 1)

    anywhere = pl.BlockSpec(memory_space=pltpu.HBM)
    span_shape = jax.ShapeDtypeStruct((span_rows, tokens), jnp.bfloat16)
    sent_rows, near_rows = pl.pallas_call(
        functools.partial(prepare_kernel, tiles_here=tiles_here),
        out_shape=[
            jax.ShapeDtypeStruct((span_rows + width, tokens), jnp.bfloat16), span_shape,
        ],
        in_specs=[anywhere] * 2,
        out_specs=vmem(2),
        scratch_shapes=[pltpu.SemaphoreType.DMA((2 + width // tokens,))],
        name="prepare",
    )(act, cotangent)
    sent_far = swap(sent_rows, "tok", 1)
    mine_far, mine_near = pl.pallas_call(
        functools.partial(mine_kernel, tiles_here=tiles_here, col_tiles=col_tiles),
        out_shape=[span_shape] * 2,
        in_specs=[anywhere],
        out_specs=vmem(2),
        scratch_shapes=[pltpu.SemaphoreType.DMA((2,))],
        name="mine",
    )(act)
    share = TILE * TILE // replicas
    listed = chosen[0, 0].astype(jnp.bfloat16)
    pad_rows = -(tiles_here + 1) % 8 + 1
    piece = jnp.concatenate(
        [
            lax.dynamic_slice(weight_tiles, (0, rep * share), (tiles_here, share)),
            jnp.zeros((pad_rows, share), jnp.bfloat16).at[0, :slots].set(listed),
        ],
        axis=0,
    )[None]
    piece_far = swap(piece, "tok", 2)
    pair = jnp.concatenate([piece, piece_far], axis=0)
    pieces = jnp.concatenate([pair, swap(pair, "tok", 1)], axis=0)
    sent_near = swap(near_rows, "tok", 1)
    far_chosen = piece_far[0, tiles_here, :slots].astype(jnp.int32)
    grid_scratch = [
        pltpu.VMEM((width // LANES, 2 * TILE, LANES), jnp.float32),
        pltpu.VMEM((spans * col_tiles * KEEP, LANES), jnp.float32),
    ]
    cuts = [tiles_here * 8 // 15, tiles_here // 9]
    cuts.append(tiles_here - sum(cuts))
    far_low, *far_sums = pl.pallas_call(
        functools.partial(far_kernel, scale=scale, spans=spans, tiles_here=tiles_here),
        out_shape=[jax.ShapeDtypeStruct((slots // 4 * KEEP, LANES), jnp.float32)]
        + [jax.ShapeDtypeStruct((n * KEEP, LANES), jnp.bfloat16) for n in cuts],
        in_specs=smem(1) + vmem(5),
        out_specs=vmem(1 + len(cuts)),
        scratch_shapes=grid_scratch,
        name="far",
    )(far_chosen, mine_far, cotangent, sent_far, split, into)
    low_from = swap(far_low, "tok", 2)
    sums_from = []
    for part in far_sums:
        sums_from.append(swap(part, "tok", 2))

    moment = momentum.reshape(tiles_here * KEEP, LANES)
    own_part, quads = pl.pallas_call(
        functools.partial(own_kernel, scale=scale, spans=spans, tiles_here=tiles_here),
        out_shape=(
            jax.ShapeDtypeStruct((tiles_here * KEEP, LANES), jnp.bfloat16),
            jax.ShapeDtypeStruct((slots // 4 * KEEP, LANES), jnp.bfloat16),
        ),
        in_specs=smem(2) + vmem(4) + [anywhere] + vmem(5),
        out_specs=tuple(vmem(2)),
        scratch_shapes=grid_scratch
        + [pltpu.VMEM((slots, KEEP, LANES), jnp.float32), pltpu.SemaphoreType.DMA((slots,))],
        name="own",
    )(
        counts[0], chosen[0, 0], mine_near, cotangent, sent_far, sent_near, moment, low_from,
        split, into, split_back, back,
    )
    new_momentum = pl.pallas_call(
        finish_kernel,
        out_shape=jax.ShapeDtypeStruct(moment.shape, jnp.float32),
        in_specs=vmem(2 + len(cuts)),
        out_specs=vmem(1)[0],
        name="finish",
    )(moment, own_part, *sums_from).reshape(momentum.shape)

    whole = jnp.concatenate(
        [
            lax.dynamic_index_in_dim(pieces, place_of(me ^ n), 0, False)[:tiles_here]
            for n in range(shards)
        ],
        axis=0,
    )
    rows_share = TILE // replicas
    matrix = whole.reshape(row_tiles, col_tiles, rows_share, TILE).transpose(0, 2, 1, 3)
    matrix = matrix.reshape(row_tiles * rows_share, width)
    list_rows = jnp.zeros((8, width), jnp.bfloat16)
    list_rows = list_rows.at[:shards, :slots].set(pieces[:, tiles_here, :slots])
    held = {0: jnp.concatenate([matrix, list_rows], axis=0)}
    cut = held[0].shape[0] // 2
    held[2] = swap(held[0], "replica", 2)
    held[4] = swap(held[0], "replica", 4)
    six = [swap(held[2][:cut], "replica", 4)]
    six.append(swap(held[4][cut:], "replica", 2))
    near = [held[0], held[2], held[4], *six]
    held_all = near + [swap(h, "replica", 1) for h in near]
    by_share = inputs.reshape(row_tiles, replicas, rows_share, tokens)
    mine = pl.pallas_call(
        reorder_kernel,
        out_shape=jax.ShapeDtypeStruct(
            (replicas, held[0].shape[0] // rows_share, rows_share, tokens), jnp.bfloat16
        ),
        in_specs=smem(1) + [anywhere],
        out_specs=vmem(1)[0],
        scratch_shapes=[pltpu.SemaphoreType.DMA((replicas,))],
        name="reorder",
    )(rep ^ jnp.asarray(SHARE_ORDER, jnp.int32), by_share)
    unchanged, places = pl.pallas_call(
        functools.partial(
            unchanged_kernel, tiles_here=tiles_here, list_row=matrix.shape[0]
        ),
        out_shape=[
            jax.ShapeDtypeStruct((tokens, width), jnp.float32),
            jax.ShapeDtypeStruct((replicas, LANES), jnp.int32),
        ],
        in_specs=vmem(1 + len(held_all)),
        out_specs=vmem(2),
        name="unchanged",
    )(mine.reshape(-1, tokens), *held_all)

    low = low_rows().astype(np.float32)
    at_once = 5
    sum_rows = -(-row_tiles * KEEP // LANES) * LANES
    along = np.kron(np.eye(at_once, dtype=np.float32), low)
    along_high, along_low = split_bf16(along)
    lows = pl.pallas_call(
        functools.partial(lows_kernel, span=at_once * TILE),
        out_shape=jax.ShapeDtypeStruct((tokens, sum_rows), jnp.bfloat16),
        in_specs=vmem(3),
        out_specs=vmem(1)[0],
        scratch_shapes=[pltpu.VMEM((sum_rows, tokens), jnp.float32)],
        name="lows",
    )(inputs, along_high, along_low)

    two = jnp.concatenate([quads[None], swap(quads[None], "tok", 2)], axis=0)
    four = jnp.concatenate([two, swap(two, "tok", 1)], axis=0)
    brought = {0: four}
    brought[2] = swap(four, "replica", 2)
    brought[4] = swap(four, "replica", 4)
    brought[6] = swap(brought[2], "replica", 4)
    for o in (0, 2, 4, 6):
        brought[o ^ 1] = swap(brought[o], "replica", 1)
    early = len(SHARE_ORDER) - 2
    begun = pl.pallas_call(
        functools.partial(begin_kernel, at=range(early)),
        out_shape=jax.ShapeDtypeStruct((col_tiles // 4 * sum_rows, LANES), jnp.float32),
        in_specs=smem(1) + vmem(early),
        out_specs=vmem(1)[0],
        compiler_params=room(12),
        name="begin",
    )(places, *[brought[o] for o in SHARE_ORDER[:early]])
    across = np.kron(np.eye(col_tiles, dtype=np.float32), low).astype(jnp.bfloat16)
    values = pl.pallas_call(
        functools.partial(last_kernel, at=range(early, len(SHARE_ORDER))),
        out_shape=jax.ShapeDtypeStruct((tokens, width), jnp.bfloat16),
        in_specs=smem(1) + vmem(4 + len(SHARE_ORDER) - early),
        out_specs=vmem(1)[0],
        scratch_shapes=[pltpu.VMEM(begun.shape, jnp.float32)],
        compiler_params=room(12),
        name="last",
    )(places, lows, unchanged, across, begun, *[brought[o] for o in SHARE_ORDER[early:]])
    return (values, new_momentum)


def solution(mesh):
    return jax.shard_map(
        local,
        mesh=mesh,
        in_specs=(
            P(("replica", "tok"), None),
            P(("replica", "tok"), None),
            P(("replica", "tok"), None),
            P("tok", None),
            P("replica", "tok", None),
            P("replica", "tok", None),
            P("replica", "tok"),
        ),
        out_specs=(P(("replica", "tok"), None), P("replica", "tok", None)),
        check_vma=False,
    )
```

profile of v0, /device:TPU:0, one launch (start us, length us, event | category | flops | bytes accessed | tf_op | source)
XLA Modules:
  0.0 113.4 jit_solution(4021786410823030358)
XLA Ops:
  0.6 0.0 copy-start
  0.7 0.7 convert_bitcast_fusion
  1.4 0.4 copy-done
  1.8 4.1 %collective-permute-start = (bf16[1,96,512]{2,1,0:T(8,128)(2,1)S(1)}, bf16[1,96,512]{2,1,0:T(8,128)(2,1)S(1)}, u32[]{:S(2)}, u32[]{:S(2)}) collective-permute-start(bf16[1,96,512]{2,1,0:T(8,128)(2,1)S(1)} %fusion.4), channel_id=1, source_target_pairs={{0,2},{1,3},{2,0},{3,1},{4,6},{5,7},{6,4},{7,5},{8,10},{9,11},{10,... | collective-permute-start | bytes 294920 | tf_op jit(solution)/shard_map/ppermute | solution.py:423
  5.9 4.9 %collective-permute-done = bf16[1,96,512]{2,1,0:T(8,128)(2,1)S(1)} collective-permute-done((bf16[1,96,512]{2,1,0:T(8,128)(2,1)S(1)}, bf16[1,96,512]{2,1,0:T(8,128)(2,1)S(1)}, u32[]{:S(2)}, u32[]{:S(2)}) %collective-permute-start) | collective-permute-done | bytes 98336 | tf_op jit(solution)/shard_map/ppermute | solution.py:423
  10.9 0.8 collective-permute-start.1
  11.6 2.2 %prepare.1 = (bf16[1280,256]{1,0:T(8,128)(2,1)}, bf16[768,256]{1,0:T(8,128)(2,1)}) custom-call(bf16[2880,256]{1,0:T(8,128)(2,1)} %bitcast.39, bf16[256,512]{1,0:T(8,128)(2,1)} %cot_ref.5), custom_call_target="tpu_custom_call" | custom-call | tf_op jit(solution)/shard_map/prepare/pallas_call | solution.py:488
  13.9 1.4 %collective-permute-start.11 = (bf16[1280,256]{1,0:T(8,128)(2,1)}, bf16[1280,256]{1,0:T(8,128)(2,1)S(1)}, u32[]{:S(2)}, u32[]{:S(2)}) collective-permute-start(bf16[1280,256]{1,0:T(8,128)(2,1)} %get-tuple-element.41), channel_id=1, source_target_pairs={{0,1},{1,0},{2,3},{3,2},{4,5},{5,4},{6,7},{7,6},{8,9},{9,8},{10,11... | collective-permute-start | bytes 1966088 | tf_op jit(solution)/shard_map/ppermute | solution.py:423
  15.2 0.7 collective-permute-start.12
  15.9 2.0 %mine.1 = (bf16[768,256]{1,0:T(8,128)(2,1)}, bf16[768,256]{1,0:T(8,128)(2,1)}) custom-call(bf16[2880,256]{1,0:T(8,128)(2,1)} %bitcast.40), custom_call_target="tpu_custom_call" | custom-call | tf_op jit(solution)/shard_map/mine/pallas_call | solution.py:499
  18.1 0.1 pad_maximum_fusion.1
  18.2 0.4 reshape.95
  18.6 0.1 copy.24
  18.7 0.4 reshape.96
  19.2 1.6 %collective-permute-start.3 = (bf16[368,512]{1,0:T(8,128)(2,1)S(1)}, bf16[368,512]{1,0:T(8,128)(2,1)S(1)}, u32[]{:S(2)}, u32[]{:S(2)}) collective-permute-start(bf16[368,512]{1,0:T(8,128)(2,1)S(1)} %fusion.1.refs_0_), channel_id=1, source_target_pairs={{0,16},{4,20},{8,24},{12,28},{16,0},{20,4},{24,8},{28,12},{1,17},{... | collective-permute-start | bytes 1130504 | tf_op jit(solution)/shard_map/ppermute | solution.py:423
  20.8 1.5 %collective-permute-start.2 = (bf16[368,512]{1,0:T(8,128)(2,1)S(1)}, bf16[368,512]{1,0:T(8,128)(2,1)S(1)}, u32[]{:S(2)}, u32[]{:S(2)}) collective-permute-start(bf16[368,512]{1,0:T(8,128)(2,1)S(1)} %fusion.1.refs_0_), channel_id=1, source_target_pairs={{0,8},{4,12},{8,0},{12,4},{16,24},{20,28},{24,16},{28,20},{1,9},{5... | collective-permute-start | bytes 1130504 | tf_op jit(solution)/shard_map/ppermute | solution.py:423
  22.3 0.5 fusion.5.chosen_ref
  22.8 8.9 %collective-permute-done.11.sent_ref = bf16[1280,256]{1,0:T(8,128)(2,1)S(1)} collective-permute-done((bf16[1280,256]{1,0:T(8,128)(2,1)}, bf16[1280,256]{1,0:T(8,128)(2,1)S(1)}, u32[]{:S(2)}, u32[]{:S(2)}) %collective-permute-start.11) | collective-permute-done | bytes 655392 | tf_op jit(solution)/shard_map/ppermute | solution.py:423
  31.7 0.8 copy-done.6
  32.6 3.1 %far.1 = (f32[64,128]{1,0:T(8,128)}, bf16[1536,128]{1,0:T(8,128)(2,1)}, bf16[320,128]{1,0:T(8,128)(2,1)}, bf16[1024,128]{1,0:T(8,128)(2,1)}) custom-call(s32[8]{0:T(128)} %fusion.5.chosen_ref, bf16[768,256]{1,0:T(8,128)(2,1)} %get-tuple-element.43.act_ref, bf16[256,512]{1,0:T(8,128)(2,1)} %cot_ref.5, bf16[1280,256]{1,0:T(8,128)(2,1)} %copy-done.6, ...), custom_call_target="tpu_custom_call" | custom-call | tf_op jit(solution)/shard_map/far/pallas_call | solution.py:528
  35.6 3.4 %collective-permute-start.13 = (f32[64,128]{1,0:T(8,128)}, f32[64,128]{1,0:T(8,128)S(1)}, u32[]{:S(2)}, u32[]{:S(2)}) collective-permute-start(f32[64,128]{1,0:T(8,128)} %get-tuple-element.44), channel_id=1, source_target_pairs={{0,2},{1,3},{2,0},{3,1},{4,6},{5,7},{6,4},{7,5},{8,10},{9,11},{10,... | collective-permute-start | bytes 98312 | tf_op jit(solution)/shard_map/ppermute | solution.py:423
  39.7 0.3 collective-permute-done.12.near_ref
  39.9 1.3 %collective-permute-done.13.far_low_ref = f32[64,128]{1,0:T(8,128)S(1)} collective-permute-done((f32[64,128]{1,0:T(8,128)}, f32[64,128]{1,0:T(8,128)S(1)}, u32[]{:S(2)}, u32[]{:S(2)}) %collective-permute-start.13) | collective-permute-done | bytes 32800 | tf_op jit(solution)/shard_map/ppermute | solution.py:423
  41.2 0.6 copy-done.18
  41.8 4.4 %own.1 = (bf16[2880,128]{1,0:T(8,128)(2,1)}, bf16[64,128]{1,0:T(8,128)(2,1)}) custom-call(s32[1]{0:T(128)} %bitcast.35.count_ref, s32[8]{0:T(128)} %bitcast.49, bf16[768,256]{1,0:T(8,128)(2,1)} %get-tuple-element.40.act_ref, bf16[256,512]{1,0:T(8,128)(2,1)} %cot_ref.5, bf16[1280,256]{1,0:T(8,128)(2,1)} %copy-done.6, ...), custom_call_target="tpu_custom_call" | custom-call | tf_op jit(solution)/shard_map/own/pallas_call | solution.py:543
  46.2 2.9 %collective-permute-start.14 = (bf16[1,64,128]{2,1,0:T(8,128)(2,1)}, bf16[1,64,128]{2,1,0:T(8,128)(2,1)S(1)}, u32[]{:S(2)}, u32[]{:S(2)}) collective-permute-start(bf16[1,64,128]{2,1,0:T(8,128)(2,1)} %bitcast.45), channel_id=1, source_target_pairs={{0,2},{1,3},{2,0},{3,1},{4,6},{5,7},{6,4},{7,5},{8,10},{9,11},{10,... | collective-permute-start | bytes 49160 | tf_op jit(solution)/shard_map/ppermute | solution.py:423
  49.1 2.0 %collective-permute-done.14 = bf16[1,64,128]{2,1,0:T(8,128)(2,1)S(1)} collective-permute-done((bf16[1,64,128]{2,1,0:T(8,128)(2,1)}, bf16[1,64,128]{2,1,0:T(8,128)(2,1)S(1)}, u32[]{:S(2)}, u32[]{:S(2)}) %collective-permute-start.14) | collective-permute-done | bytes 16416 | tf_op jit(solution)/shard_map/ppermute | solution.py:423
  51.1 0.7 pad_maximum_fusion.4
  51.8 2.1 %collective-permute-start.15 = (bf16[2,64,128]{2,1,0:T(8,128)(2,1)S(1)}, bf16[2,64,128]{2,1,0:T(8,128)(2,1)S(1)}, u32[]{:S(2)}, u32[]{:S(2)}) collective-permute-start(bf16[2,64,128]{2,1,0:T(8,128)(2,1)S(1)} %pad_maximum_fusion.4), channel_id=1, source_target_pairs={{0,1},{1,0},{2,3},{3,2},{4,5},{5,4},{6,7},{7,6},{8,9},{9,8},{10,11... | collective-permute-start | bytes 98312 | tf_op jit(solution)/shard_map/ppermute | solution.py:423
  53.9 1.9 %collective-permute-done.15 = bf16[2,64,128]{2,1,0:T(8,128)(2,1)S(1)} collective-permute-done((bf16[2,64,128]{2,1,0:T(8,128)(2,1)S(1)}, bf16[2,64,128]{2,1,0:T(8,128)(2,1)S(1)}, u32[]{:S(2)}, u32[]{:S(2)}) %collective-permute-start.15) | collective-permute-done | bytes 32800 | tf_op jit(solution)/shard_map/ppermute | solution.py:423
  55.8 0.7 pad_maximum_fusion.3.refs_0_
  56.5 1.5 %collective-permute-start.16 = (bf16[4,64,128]{2,1,0:T(8,128)(2,1)S(1)}, bf16[4,64,128]{2,1,0:T(8,128)(2,1)S(1)}, u32[]{:S(2)}, u32[]{:S(2)}) collective-permute-start(bf16[4,64,128]{2,1,0:T(8,128)(2,1)S(1)} %pad_maximum_fusion.3.refs_0_), channel_id=1, source_target_pairs={{0,8},{4,12},{8,0},{12,4},{16,24},{20,28},{24,16},{28,20},{1,9},{5... | collective-permute-start | bytes 196616 | tf_op jit(solution)/shard_map/ppermute | solution.py:423
  58.0 0.6 collective-permute-start.5
  58.6 0.0 collective-permute-done.2.refs_1_
  58.7 1.6 %collective-permute-start.4 = (bf16[184,512]{1,0:T(8,128)(2,1)S(1)}, bf16[184,512]{1,0:T(8,128)(2,1)S(1)}, u32[]{:S(2)}, u32[]{:S(2)}) collective-permute-start(bf16[184,512]{1,0:T(8,128)(2,1)S(1)} %slice.85), channel_id=1, source_target_pairs={{0,16},{4,20},{8,24},{12,28},{16,0},{20,4},{24,8},{28,12},{1,17},{... | collective-permute-start | bytes 565256 | tf_op jit(solution)/shard_map/ppermute | solution.py:423
  60.2 0.5 collective-permute-start.17
  60.8 0.0 collective-permute-done.6.refs_5_
  60.8 0.0 collective-permute-start.7
  60.8 0.0 collective-permute-done.16.refs_1_
  60.8 0.5 collective-permute-start.8
  61.3 3.7 %collective-permute-done.17.refs_2_ = bf16[4,64,128]{2,1,0:T(8,128)(2,1)S(1)} collective-permute-done((bf16[4,64,128]{2,1,0:T(8,128)(2,1)S(1)}, bf16[4,64,128]{2,1,0:T(8,128)(2,1)S(1)}, u32[]{:S(2)}, u32[]{:S(2)}) %collective-permute-start.17) | collective-permute-done | bytes 65568 | tf_op jit(solution)/shard_map/ppermute | solution.py:423
  65.0 1.3 %collective-permute-done.18.refs_3_ = bf16[4,64,128]{2,1,0:T(8,128)(2,1)S(1)} collective-permute-done((bf16[4,64,128]{2,1,0:T(8,128)(2,1)S(1)}, bf16[4,64,128]{2,1,0:T(8,128)(2,1)S(1)}, u32[]{:S(2)}, u32[]{:S(2)}) %collective-permute-start.18) | collective-permute-done | bytes 65568 | tf_op jit(solution)/shard_map/ppermute | solution.py:423
  66.3 0.2 collective-permute-start.19
  66.4 1.5 %collective-permute-start.21 = (bf16[4,64,128]{2,1,0:T(8,128)(2,1)S(1)}, bf16[4,64,128]{2,1,0:T(8,128)(2,1)S(1)}, u32[]{:S(2)}, u32[]{:S(2)}) collective-permute-start(bf16[4,64,128]{2,1,0:T(8,128)(2,1)S(1)} %collective-permute-done.16.refs_1_), channel_id=1, source_target_pairs={{0,16},{4,20},{8,24},{12,28},{16,0},{20,4},{24,8},{28,12},{1,17},{... | collective-permute-start | bytes 196616 | tf_op jit(solution)/shard_map/ppermute | solution.py:423
  68.0 0.1 collective-permute-start.10
  68.0 0.4 collective-permute-start.9
  68.5 2.3 %collective-permute-done.21.refs_0_ = bf16[4,64,128]{2,1,0:T(8,128)(2,1)S(1)} collective-permute-done((bf16[4,64,128]{2,1,0:T(8,128)(2,1)S(1)}, bf16[4,64,128]{2,1,0:T(8,128)(2,1)S(1)}, u32[]{:S(2)}, u32[]{:S(2)}) %collective-permute-start.21) | collective-permute-done | bytes 65568 | tf_op jit(solution)/shard_map/ppermute | solution.py:423
  70.8 2.8 %collective-permute-start.23 = (bf16[1536,128]{1,0:T(8,128)(2,1)}, bf16[1536,128]{1,0:T(8,128)(2,1)}, u32[]{:S(2)}, u32[]{:S(2)}) collective-permute-start(bf16[1536,128]{1,0:T(8,128)(2,1)} %get-tuple-element.47), channel_id=1, source_target_pairs={{0,2},{1,3},{2,0},{3,1},{4,6},{5,7},{6,4},{7,5},{8,10},{9,11},{10,... | collective-permute-start | bytes 1179656 | tf_op jit(solution)/shard_map/ppermute | solution.py:423
  73.6 0.1 collective-permute-start.25
  73.7 2.8 %collective-permute-start.24 = (bf16[320,128]{1,0:T(8,128)(2,1)}, bf16[320,128]{1,0:T(8,128)(2,1)S(1)}, u32[]{:S(2)}, u32[]{:S(2)}) collective-permute-start(bf16[320,128]{1,0:T(8,128)(2,1)} %get-tuple-element.48), channel_id=1, source_target_pairs={{0,2},{1,3},{2,0},{3,1},{4,6},{5,7},{6,4},{7,5},{8,10},{9,11},{10,... | collective-permute-start | bytes 245768 | tf_op jit(solution)/shard_map/ppermute | solution.py:423
  76.5 0.1 collective-permute-start.20
  76.6 0.8 copy-done.12
  77.4 0.5 collective-permute-start.22
  77.9 0.5 broadcast_xor_fusion.order_ref
  78.3 3.3 %reorder.1 = bf16[8,46,8,256]{3,2,1,0:T(8,128)(2,1)} custom-call(s32[8]{0:T(128)} %broadcast_xor_fusion.order_ref, bf16[45,8,8,256]{3,2,1,0:T(8,128)(2,1)} %bitcast.37), custom_call_target="tpu_custom_call" | custom-call | tf_op jit(solution)/shard_map/reorder/pallas_call | solution.py:587
  81.7 3.4 %lows.1.lows_ref = bf16[256,1536]{1,0:T(8,128)(2,1)} custom-call(bf16[2880,256]{1,0:T(8,128)(2,1)} %bitcast.38, bf16[160,320]{1,0:T(8,128)(2,1)} %constant.102.clone.high_ref, bf16[160,320]{1,0:T(8,128)(2,1)} %constant.103.clone.low_ref), custom_call_target="tpu_custom_call" | custom-call | tf_op jit(solution)/shard_map/lows/pallas_call | solution.py:615
  85.1 4.3 %unchanged.1 = (f32[256,512]{1,0:T(8,128)}, s32[8,128]{1,0:T(8,128)}) custom-call(bf16[2944,256]{1,0:T(8,128)(2,1)} %bitcast.36, bf16[368,512]{1,0:T(8,128)(2,1)} %copy-done.7, bf16[368,512]{1,0:T(8,128)(2,1)} %copy-done.9, bf16[368,512]{1,0:T(8,128)(2,1)} %copy-done.8, bf16[184,512]{1,0:T(8,128)(2,1)} %copy-done.14, bf16[184,512]{1,0:T(8,128)(2,1)} %copy-done.13, ...), custom_call_target="tpu_custom_call" | custom-call | tf_op jit(solution)/shard_map/unchanged/pallas_call | solution.py:597
  89.4 0.7 copy-done.4
  90.1 2.8 %begin.1.begun_ref = f32[3072,128]{1,0:T(8,128)S(1)} custom-call(s32[8,128]{1,0:T(8,128)S(1)} %copy-done.4, bf16[4,64,128]{2,1,0:T(8,128)(2,1)S(1)} %pad_maximum_fusion.3.refs_0_, bf16[4,64,128]{2,1,0:T(8,128)(2,1)S(1)} %collective-permute-done.16.refs_1_, bf16[4,64,128]{2,1,0:T(8,128)(2,1)S(1)} %collective-permute-done.17.refs_2_, ...), custom_call_target="tpu_custom_call" | custom-call | tf_op jit(solution)/shard_map/begin/pallas_call | solution.py:633
  92.9 12.8 %collective-permute-done.24.refs_1_ = bf16[320,128]{1,0:T(8,128)(2,1)S(1)} collective-permute-done((bf16[320,128]{1,0:T(8,128)(2,1)}, bf16[320,128]{1,0:T(8,128)(2,1)S(1)}, u32[]{:S(2)}, u32[]{:S(2)}) %collective-permute-start.24) | collective-permute-done | bytes 81952 | tf_op jit(solution)/shard_map/ppermute | solution.py:423
  105.7 0.6 copy-done.17
  106.4 3.2 %finish.1 = f32[2880,128]{1,0:T(8,128)} custom-call(f32[2880,128]{1,0:T(8,128)} %bitcast.42, bf16[2880,128]{1,0:T(8,128)(2,1)} %get-tuple-element.46.part_ref, bf16[1536,128]{1,0:T(8,128)(2,1)} %collective-permute-done.23.refs_0_, bf16[320,128]{1,0:T(8,128)(2,1)} %copy-done.17, bf16[1024,128]{1,0:T(8,128)(2,1)} %collective-permute-done.25.refs_2_), custom_call_target="tpu_custom_call" | custom-call | tf_op jit(solution)/shard_map/finish/pallas_call | solution.py:558
  109.6 1.0 copy-done.2
  110.6 2.7 %last.1 = bf16[256,512]{1,0:T(8,128)(2,1)} custom-call(s32[8,128]{1,0:T(8,128)S(1)} %copy-done.5, bf16[256,1536]{1,0:T(8,128)(2,1)S(1)} %copy-done.1, f32[256,512]{1,0:T(8,128)S(1)} %copy-done.2, bf16[256,512]{1,0:T(8,128)(2,1)S(1)} %copy-done.3, f32[3072,128]{1,0:T(8,128)S(1)} %begin.1.begun_ref, bf16[4,64,128]{2,1,0:T(8,128)(2,1)S(1)} %collective-permute-done.21.refs_0_, ...), custom_call_target="tpu_custom_call" | custom-call | tf_op jit(solution)/shard_map/last/pallas_call | solution.py:642
  (57 shorter events, 0.3 us)
Async XLA Ops:
  0.6 1.2 %copy-start = (bf16[90,4096]{1,0:T(8,128)(2,1)S(1)}, bf16[90,4096]{1,0:T(8,128)(2,1)}, u32[]{:S(2)}) copy-start(bf16[90,4096]{1,0:T(8,128)(2,1)} %param.22) | copy-start | bytes 2211844
  1.8 9.0 %collective-permute-start = (bf16[1,96,512]{2,1,0:T(8,128)(2,1)S(1)}, bf16[1,96,512]{2,1,0:T(8,128)(2,1)S(1)}, u32[]{:S(2)}, u32[]{:S(2)}) collective-permute-start(bf16[1,96,512]{2,1,0:T(8,128)(2,1)S(1)} %fusion.4), channel_id=1, source_target_pairs={{0,2},{1,3},{2,0},{3,1},{4,6},{5,7},{6,4},{7,5},{8,10},{9,11},{10,... | collective-permute-start | bytes 294920 | tf_op jit(solution)/shard_map/ppermute | solution.py:423
  10.9 7.1 %collective-permute-start.1 = (bf16[2,96,512]{2,1,0:T(8,128)(2,1)S(1)}, bf16[2,96,512]{2,1,0:T(8,128)(2,1)S(1)}, u32[]{:S(2)}, u32[]{:S(2)}) collective-permute-start(bf16[2,96,512]{2,1,0:T(8,128)(2,1)S(1)} %pad_maximum_fusion.2), channel_id=1, source_target_pairs={{0,1},{1,0},{2,3},{3,2},{4,5},{5,4},{6,7},{7,6},{8,9},{9,8},{10,11... | collective-permute-start | bytes 589832 | tf_op jit(solution)/shard_map/ppermute | solution.py:423
  13.9 17.9 %collective-permute-start.11 = (bf16[1280,256]{1,0:T(8,128)(2,1)}, bf16[1280,256]{1,0:T(8,128)(2,1)S(1)}, u32[]{:S(2)}, u32[]{:S(2)}) collective-permute-start(bf16[1280,256]{1,0:T(8,128)(2,1)} %get-tuple-element.41), channel_id=1, source_target_pairs={{0,1},{1,0},{2,3},{3,2},{4,5},{5,4},{6,7},{7,6},{8,9},{9,8},{10,11... | collective-permute-start | bytes 1966088 | tf_op jit(solution)/shard_map/ppermute | solution.py:423
  15.2 24.7 %collective-permute-start.12 = (bf16[768,256]{1,0:T(8,128)(2,1)}, bf16[768,256]{1,0:T(8,128)(2,1)}, u32[]{:S(2)}, u32[]{:S(2)}) collective-permute-start(bf16[768,256]{1,0:T(8,128)(2,1)} %get-tuple-element.42), channel_id=1, source_target_pairs={{0,1},{1,0},{2,3},{3,2},{4,5},{5,4},{6,7},{7,6},{8,9},{9,8},{10,11... | collective-permute-start | bytes 1179656 | tf_op jit(solution)/shard_map/ppermute | solution.py:423
  19.2 62.5 %copy-start.7 = (bf16[368,512]{1,0:T(8,128)(2,1)}, bf16[368,512]{1,0:T(8,128)(2,1)S(1)}, u32[]{:S(2)}) copy-start(bf16[368,512]{1,0:T(8,128)(2,1)S(1)} %fusion.1.refs_0_) | copy-start | bytes 1130500
  19.2 38.8 %collective-permute-start.3 = (bf16[368,512]{1,0:T(8,128)(2,1)S(1)}, bf16[368,512]{1,0:T(8,128)(2,1)S(1)}, u32[]{:S(2)}, u32[]{:S(2)}) collective-permute-start(bf16[368,512]{1,0:T(8,128)(2,1)S(1)} %fusion.1.refs_0_), channel_id=1, source_target_pairs={{0,16},{4,20},{8,24},{12,28},{16,0},{20,4},{24,8},{28,12},{1,17},{... | collective-permute-start | bytes 1130504 | tf_op jit(solution)/shard_map/ppermute | solution.py:423
  20.8 37.8 %collective-permute-start.2 = (bf16[368,512]{1,0:T(8,128)(2,1)S(1)}, bf16[368,512]{1,0:T(8,128)(2,1)S(1)}, u32[]{:S(2)}, u32[]{:S(2)}) collective-permute-start(bf16[368,512]{1,0:T(8,128)(2,1)S(1)} %fusion.1.refs_0_), channel_id=1, source_target_pairs={{0,8},{4,12},{8,0},{12,4},{16,24},{20,28},{24,16},{28,20},{1,9},{5... | collective-permute-start | bytes 1130504 | tf_op jit(solution)/shard_map/ppermute | solution.py:423
  22.3 38.5 %collective-permute-start.6 = (bf16[368,512]{1,0:T(8,128)(2,1)S(1)}, bf16[368,512]{1,0:T(8,128)(2,1)S(1)}, u32[]{:S(2)}, u32[]{:S(2)}) collective-permute-start(bf16[368,512]{1,0:T(8,128)(2,1)S(1)} %fusion.1.refs_0_), channel_id=1, source_target_pairs={{0,4},{4,0},{8,12},{12,8},{16,20},{20,16},{24,28},{28,24},{1,5},{5... | collective-permute-start | bytes 1130504 | tf_op jit(solution)/shard_map/ppermute | solution.py:423
  31.7 0.8 copy-start.6
  35.6 5.5 %collective-permute-start.13 = (f32[64,128]{1,0:T(8,128)}, f32[64,128]{1,0:T(8,128)S(1)}, u32[]{:S(2)}, u32[]{:S(2)}) collective-permute-start(f32[64,128]{1,0:T(8,128)} %get-tuple-element.44), channel_id=1, source_target_pairs={{0,2},{1,3},{2,0},{3,1},{4,6},{5,7},{6,4},{7,5},{8,10},{9,11},{10,... | collective-permute-start | bytes 98312 | tf_op jit(solution)/shard_map/ppermute | solution.py:423
  41.2 0.6 copy-start.18
  41.8 36.1 %copy-start.19 = (s32[8]{0:T(128)S(1)}, s32[8]{0:T(128)}, u32[]{:S(2)}) copy-start(s32[8]{0:T(128)} %constant.101.clone) | copy-start | bytes 100
  46.2 4.9 %collective-permute-start.14 = (bf16[1,64,128]{2,1,0:T(8,128)(2,1)}, bf16[1,64,128]{2,1,0:T(8,128)(2,1)S(1)}, u32[]{:S(2)}, u32[]{:S(2)}) collective-permute-start(bf16[1,64,128]{2,1,0:T(8,128)(2,1)} %bitcast.45), channel_id=1, source_target_pairs={{0,2},{1,3},{2,0},{3,1},{4,6},{5,7},{6,4},{7,5},{8,10},{9,11},{10,... | collective-permute-start | bytes 49160 | tf_op jit(solution)/shard_map/ppermute | solution.py:423
  51.8 4.0 %collective-permute-start.15 = (bf16[2,64,128]{2,1,0:T(8,128)(2,1)S(1)}, bf16[2,64,128]{2,1,0:T(8,128)(2,1)S(1)}, u32[]{:S(2)}, u32[]{:S(2)}) collective-permute-start(bf16[2,64,128]{2,1,0:T(8,128)(2,1)S(1)} %pad_maximum_fusion.4), channel_id=1, source_target_pairs={{0,1},{1,0},{2,3},{3,2},{4,5},{5,4},{6,7},{7,6},{8,9},{9,8},{10,11... | collective-permute-start | bytes 98312 | tf_op jit(solution)/shard_map/ppermute | solution.py:423
  56.5 4.3 %collective-permute-start.16 = (bf16[4,64,128]{2,1,0:T(8,128)(2,1)S(1)}, bf16[4,64,128]{2,1,0:T(8,128)(2,1)S(1)}, u32[]{:S(2)}, u32[]{:S(2)}) collective-permute-start(bf16[4,64,128]{2,1,0:T(8,128)(2,1)S(1)} %pad_maximum_fusion.3.refs_0_), channel_id=1, source_target_pairs={{0,8},{4,12},{8,0},{12,4},{16,24},{20,28},{24,16},{28,20},{1,9},{5... | collective-permute-start | bytes 196616 | tf_op jit(solution)/shard_map/ppermute | solution.py:423
  58.0 23.7 %copy-start.8 = (bf16[368,512]{1,0:T(8,128)(2,1)}, bf16[368,512]{1,0:T(8,128)(2,1)S(1)}, u32[]{:S(2)}) copy-start(bf16[368,512]{1,0:T(8,128)(2,1)S(1)} %collective-permute-done.3.refs_2_) | copy-start | bytes 1130500
  58.0 8.4 %collective-permute-start.5 = (bf16[184,512]{1,0:T(8,128)(2,1)S(1)}, bf16[184,512]{1,0:T(8,128)(2,1)S(1)}, u32[]{:S(2)}, u32[]{:S(2)}) collective-permute-start(bf16[184,512]{1,0:T(8,128)(2,1)S(1)} %slice.86), channel_id=1, source_target_pairs={{0,8},{4,12},{8,0},{12,4},{16,24},{20,28},{24,16},{28,20},{1,9},{5... | collective-permute-start | bytes 565256 | tf_op jit(solution)/shard_map/ppermute | solution.py:423
  58.6 23.1 %copy-start.9 = (bf16[368,512]{1,0:T(8,128)(2,1)}, bf16[368,512]{1,0:T(8,128)(2,1)S(1)}, u32[]{:S(2)}) copy-start(bf16[368,512]{1,0:T(8,128)(2,1)S(1)} %collective-permute-done.2.refs_1_) | copy-start | bytes 1130500
  58.7 9.3 %collective-permute-start.4 = (bf16[184,512]{1,0:T(8,128)(2,1)S(1)}, bf16[184,512]{1,0:T(8,128)(2,1)S(1)}, u32[]{:S(2)}, u32[]{:S(2)}) collective-permute-start(bf16[184,512]{1,0:T(8,128)(2,1)S(1)} %slice.85), channel_id=1, source_target_pairs={{0,16},{4,20},{8,24},{12,28},{16,0},{20,4},{24,8},{28,12},{1,17},{... | collective-permute-start | bytes 565256 | tf_op jit(solution)/shard_map/ppermute | solution.py:423
  60.2 4.8 %collective-permute-start.17 = (bf16[4,64,128]{2,1,0:T(8,128)(2,1)S(1)}, bf16[4,64,128]{2,1,0:T(8,128)(2,1)S(1)}, u32[]{:S(2)}, u32[]{:S(2)}) collective-permute-start(bf16[4,64,128]{2,1,0:T(8,128)(2,1)S(1)} %pad_maximum_fusion.3.refs_0_), channel_id=1, source_target_pairs={{0,16},{4,20},{8,24},{12,28},{16,0},{20,4},{24,8},{28,12},{1,17},{... | collective-permute-start | bytes 196616 | tf_op jit(solution)/shard_map/ppermute | solution.py:423
  60.8 21.0 %copy-start.10 = (bf16[368,512]{1,0:T(8,128)(2,1)}, bf16[368,512]{1,0:T(8,128)(2,1)S(1)}, u32[]{:S(2)}) copy-start(bf16[368,512]{1,0:T(8,128)(2,1)S(1)} %collective-permute-done.6.refs_5_) | copy-start | bytes 1130500
  60.8 15.8 %collective-permute-start.7 = (bf16[368,512]{1,0:T(8,128)(2,1)S(1)}, bf16[368,512]{1,0:T(8,128)(2,1)S(1)}, u32[]{:S(2)}, u32[]{:S(2)}) collective-permute-start(bf16[368,512]{1,0:T(8,128)(2,1)S(1)} %collective-permute-done.2.refs_1_), channel_id=1, source_target_pairs={{0,4},{4,0},{8,12},{12,8},{16,20},{20,16},{24,28},{28,24},{1,5},{5... | collective-permute-start | bytes 1130504 | tf_op jit(solution)/shard_map/ppermute | solution.py:423
  60.8 15.8 %collective-permute-start.8 = (bf16[368,512]{1,0:T(8,128)(2,1)S(1)}, bf16[368,512]{1,0:T(8,128)(2,1)S(1)}, u32[]{:S(2)}, u32[]{:S(2)}) collective-permute-start(bf16[368,512]{1,0:T(8,128)(2,1)S(1)} %collective-permute-done.3.refs_2_), channel_id=1, source_target_pairs={{0,4},{4,0},{8,12},{12,8},{16,20},{20,16},{24,28},{28,24},{1,5},{5... | collective-permute-start | bytes 1130504 | tf_op jit(solution)/shard_map/ppermute | solution.py:423
  65.0 1.3 %collective-permute-start.18 = (bf16[4,64,128]{2,1,0:T(8,128)(2,1)S(1)}, bf16[4,64,128]{2,1,0:T(8,128)(2,1)S(1)}, u32[]{:S(2)}, u32[]{:S(2)}) collective-permute-start(bf16[4,64,128]{2,1,0:T(8,128)(2,1)S(1)} %pad_maximum_fusion.3.refs_0_), channel_id=1, source_target_pairs={{0,4},{4,0},{8,12},{12,8},{16,20},{20,16},{24,28},{28,24},{1,5},{5... | collective-permute-start | bytes 196616 | tf_op jit(solution)/shard_map/ppermute | solution.py:423
  66.3 1.8 %collective-permute-start.19 = (bf16[4,64,128]{2,1,0:T(8,128)(2,1)S(1)}, bf16[4,64,128]{2,1,0:T(8,128)(2,1)S(1)}, u32[]{:S(2)}, u32[]{:S(2)}) collective-permute-start(bf16[4,64,128]{2,1,0:T(8,128)(2,1)S(1)} %collective-permute-done.16.refs_1_), channel_id=1, source_target_pairs={{0,4},{4,0},{8,12},{12,8},{16,20},{20,16},{24,28},{28,24},{1,5},{5... | collective-permute-start | bytes 196616 | tf_op jit(solution)/shard_map/ppermute | solution.py:423
  66.4 10.1 %copy-start.13 = (bf16[184,512]{1,0:T(8,128)(2,1)}, bf16[184,512]{1,0:T(8,128)(2,1)S(1)}, u32[]{:S(2)}) copy-start(bf16[184,512]{1,0:T(8,128)(2,1)S(1)} %collective-permute-done.5.refs_4_) | copy-start | bytes 565252
  66.4 4.4 %collective-permute-start.21 = (bf16[4,64,128]{2,1,0:T(8,128)(2,1)S(1)}, bf16[4,64,128]{2,1,0:T(8,128)(2,1)S(1)}, u32[]{:S(2)}, u32[]{:S(2)}) collective-permute-start(bf16[4,64,128]{2,1,0:T(8,128)(2,1)S(1)} %collective-permute-done.16.refs_1_), channel_id=1, source_target_pairs={{0,16},{4,20},{8,24},{12,28},{16,0},{20,4},{24,8},{28,12},{1,17},{... | collective-permute-start | bytes 196616 | tf_op jit(solution)/shard_map/ppermute | solution.py:423
  68.0 8.6 %copy-start.14 = (bf16[184,512]{1,0:T(8,128)(2,1)}, bf16[184,512]{1,0:T(8,128)(2,1)S(1)}, u32[]{:S(2)}) copy-start(bf16[184,512]{1,0:T(8,128)(2,1)S(1)} %collective-permute-done.4.refs_3_) | copy-start | bytes 565252
  68.0 5.6 %collective-permute-start.10 = (bf16[184,512]{1,0:T(8,128)(2,1)S(1)}, bf16[184,512]{1,0:T(8,128)(2,1)S(1)}, u32[]{:S(2)}, u32[]{:S(2)}) collective-permute-start(bf16[184,512]{1,0:T(8,128)(2,1)S(1)} %collective-permute-done.5.refs_4_), channel_id=1, source_target_pairs={{0,4},{4,0},{8,12},{12,8},{16,20},{20,16},{24,28},{28,24},{1,5},{5... | collective-permute-start | bytes 565256 | tf_op jit(solution)/shard_map/ppermute | solution.py:423
  68.0 5.7 %collective-permute-start.9 = (bf16[184,512]{1,0:T(8,128)(2,1)S(1)}, bf16[184,512]{1,0:T(8,128)(2,1)S(1)}, u32[]{:S(2)}, u32[]{:S(2)}) collective-permute-start(bf16[184,512]{1,0:T(8,128)(2,1)S(1)} %collective-permute-done.4.refs_3_), channel_id=1, source_target_pairs={{0,4},{4,0},{8,12},{12,8},{16,20},{20,16},{24,28},{28,24},{1,5},{5... | collective-permute-start | bytes 565256 | tf_op jit(solution)/shard_map/ppermute | solution.py:423
  70.8 35.0 %collective-permute-start.23 = (bf16[1536,128]{1,0:T(8,128)(2,1)}, bf16[1536,128]{1,0:T(8,128)(2,1)}, u32[]{:S(2)}, u32[]{:S(2)}) collective-permute-start(bf16[1536,128]{1,0:T(8,128)(2,1)} %get-tuple-element.47), channel_id=1, source_target_pairs={{0,2},{1,3},{2,0},{3,1},{4,6},{5,7},{6,4},{7,5},{8,10},{9,11},{10,... | collective-permute-start | bytes 1179656 | tf_op jit(solution)/shard_map/ppermute | solution.py:423
  73.6 3.0 %copy-start.15 = (bf16[184,512]{1,0:T(8,128)(2,1)}, bf16[184,512]{1,0:T(8,128)(2,1)S(1)}, u32[]{:S(2)}) copy-start(bf16[184,512]{1,0:T(8,128)(2,1)S(1)} %collective-permute-done.10.refs_9_) | copy-start | bytes 565252
  73.6 32.2 %collective-permute-start.25 = (bf16[1024,128]{1,0:T(8,128)(2,1)}, bf16[1024,128]{1,0:T(8,128)(2,1)}, u32[]{:S(2)}, u32[]{:S(2)}) collective-permute-start(bf16[1024,128]{1,0:T(8,128)(2,1)} %get-tuple-element.49), channel_id=1, source_target_pairs={{0,2},{1,3},{2,0},{3,1},{4,6},{5,7},{6,4},{7,5},{8,10},{9,11},{10,... | collective-permute-start | bytes 786440 | tf_op jit(solution)/shard_map/ppermute | solution.py:423
  73.7 2.9 %copy-start.16 = (bf16[184,512]{1,0:T(8,128)(2,1)}, bf16[184,512]{1,0:T(8,128)(2,1)S(1)}, u32[]{:S(2)}) copy-start(bf16[184,512]{1,0:T(8,128)(2,1)S(1)} %collective-permute-done.9.refs_8_) | copy-start | bytes 565252
  73.7 32.0 %collective-permute-start.24 = (bf16[320,128]{1,0:T(8,128)(2,1)}, bf16[320,128]{1,0:T(8,128)(2,1)S(1)}, u32[]{:S(2)}, u32[]{:S(2)}) collective-permute-start(bf16[320,128]{1,0:T(8,128)(2,1)} %get-tuple-element.48), channel_id=1, source_target_pairs={{0,2},{1,3},{2,0},{3,1},{4,6},{5,7},{6,4},{7,5},{8,10},{9,11},{10,... | collective-permute-start | bytes 245768 | tf_op jit(solution)/shard_map/ppermute | solution.py:423
  76.5 5.2 %copy-start.11 = (bf16[368,512]{1,0:T(8,128)(2,1)}, bf16[368,512]{1,0:T(8,128)(2,1)S(1)}, u32[]{:S(2)}) copy-start(bf16[368,512]{1,0:T(8,128)(2,1)S(1)} %collective-permute-done.7.refs_6_) | copy-start | bytes 1130500
  76.5 12.9 %collective-permute-start.20 = (bf16[4,64,128]{2,1,0:T(8,128)(2,1)S(1)}, bf16[4,64,128]{2,1,0:T(8,128)(2,1)S(1)}, u32[]{:S(2)}, u32[]{:S(2)}) collective-permute-start(bf16[4,64,128]{2,1,0:T(8,128)(2,1)S(1)} %collective-permute-done.17.refs_2_), channel_id=1, source_target_pairs={{0,4},{4,0},{8,12},{12,8},{16,20},{20,16},{24,28},{28,24},{1,5},{5... | collective-permute-start | bytes 196616 | tf_op jit(solution)/shard_map/ppermute | solution.py:423
  76.6 0.8 copy-start.12
  77.4 32.2 %collective-permute-start.22 = (bf16[4,64,128]{2,1,0:T(8,128)(2,1)S(1)}, bf16[4,64,128]{2,1,0:T(8,128)(2,1)S(1)}, u32[]{:S(2)}, u32[]{:S(2)}) collective-permute-start(bf16[4,64,128]{2,1,0:T(8,128)(2,1)S(1)} %collective-permute-done.21.refs_0_), channel_id=1, source_target_pairs={{0,4},{4,0},{8,12},{12,8},{16,20},{20,16},{24,28},{28,24},{1,5},{5... | collective-permute-start | bytes 196616 | tf_op jit(solution)/shard_map/ppermute | solution.py:423
  89.4 0.7 copy-start.4
  105.7 0.6 copy-start.17
  106.4 3.2 %copy-start.1 = (bf16[256,1536]{1,0:T(8,128)(2,1)S(1)}, bf16[256,1536]{1,0:T(8,128)(2,1)}, u32[]{:S(2)}) copy-start(bf16[256,1536]{1,0:T(8,128)(2,1)} %lows.1.lows_ref) | copy-start | bytes 2359300
  106.4 3.2 %copy-start.3 = (bf16[256,512]{1,0:T(8,128)(2,1)S(1)}, bf16[256,512]{1,0:T(8,128)(2,1)}, u32[]{:S(2)}) copy-start(bf16[256,512]{1,0:T(8,128)(2,1)} %constant.104.clone.across_ref) | copy-start | bytes 786436
  106.4 3.2 %copy-start.5 = (s32[8,128]{1,0:T(8,128)S(1)}, s32[8,128]{1,0:T(8,128)}, u32[]{:S(2)}) copy-start(s32[8,128]{1,0:T(8,128)} %get-tuple-element.38.place_ref) | copy-start | bytes 12292
  109.6 1.0 copy-start.2
where the time goes:
time: 114 us; the launch traced here: 113 us
  waiting for transfers between devices  39.4 us (35%)
  starting transfers between devices  31.6 us (28%)
  Pallas kernels  31.4 us (28%)
  local copies, waits for them, and re-layouts  6.02 us (5%)
  other arithmetic  3.37 us (3%)
  between operations  1.6 us (1%)
    ppermute x26, waiting for transfers between devices, swap(): return lax.ppermute(array, axis, [(i, i ^ bit) for i in range(size)])  39.4 us
    ppermute x26, starting transfers between devices, swap(): return lax.ppermute(array, axis, [(i, i ^ bit) for i in range(size)])  31.6 us
    unnamed x41, local copies, waits for them, and re-layouts  4.99 us
    pallas_call x1, Pallas kernels, four_shards(): pl.pallas_call(functools.partial(own_kernel, scale=scale, spans=spans, ti...  4.36 us
    pallas_call x1, Pallas kernels, four_shards(): pl.pallas_call(functools.partial(unchanged_kernel, tiles_here=tiles_here,...  4.31 us
    pallas_call x1, Pallas kernels, four_shards(): pl.pallas_call(functools.partial(lows_kernel, span=at_once * TILE), out_s...  3.36 us
    pallas_call x1, Pallas kernels, four_shards(): pl.pallas_call(reorder_kernel, out_shape=jax.ShapeDtypeStruct((replicas,...  3.33 us
    pallas_call x1, Pallas kernels, four_shards(): pl.pallas_call(finish_kernel, out_shape=jax.ShapeDtypeStruct(moment.shape...  3.2 us
  transfers between devices with their start and end apart: 26, of which 10 were waited for; matrix products, arithmetic and copies ran while one was open for 3% of the time, Pallas kernels for 25%

commit v1 on v0

--- a/solution.py
+++ b/solution.py
@@ -22,7 +22,7 @@
 
 TOK_ORDER = (0, 2, 1, 3)
 SHARE_ORDER = (0, 2, 4, 1, 3, 5, 6, 7)
-HELD_ORDER = (0, 2, 4, 6, 6, 1, 3, 5, 7, 7)
+HELD_ORDER = (0, 2, 4, 6, 1, 3, 5, 7)
 
 
 def cosine_rows(count):
@@ -194,13 +194,11 @@
         first += rows
 
 
-def own_kernel(
-    count_ref, chosen_ref, act_ref, cot_ref, sent_ref, near_ref, mom_ref, far_low_ref,
-    split_ref, into_ref, split_back_ref, back_ref,
-    part_ref, quad_ref, grid_ref, tiled_ref, held_ref, sems, *, scale, spans, tiles_here,
+def factor_lows_kernel(
+    chosen_ref, other_ref, mom_ref, act_ref, cot_ref, along_high_ref, along_low_ref,
+    back_high_ref, back_low_ref, split_ref, into_ref,
+    mine_ref, theirs_ref, high_ref, low_ref, all_ref, held_ref, sems, *, scale, tiles_here,
 ):
-    skip = first_skip(lax.axis_index("tok"), tiles_here, cot_ref.shape[1] // TILE)
-    count = count_ref[0]
     slots = chosen_ref.shape[0]
     copies = [
         pltpu.make_async_copy(
@@ -211,35 +209,87 @@
     ]
     for copy in copies:
         copy.start()
+    span, half = along_high_ref.shape[1], along_high_ref.shape[0]
+    for c in range(act_ref.shape[0] // span):
+        piece = act_ref[c * span : (c + 1) * span, :]
+        rows = slice(c * half, (c + 1) * half)
+        whole = jnp.dot(
+            along_high_ref[...], piece, preferred_element_type=jnp.float32
+        ) + jnp.dot(along_low_ref[...], piece, preferred_element_type=jnp.float32)
+        high_ref[rows, :] = whole.astype(jnp.bfloat16)
+        low_ref[rows, :] = (whole - whole.astype(jnp.bfloat16).astype(jnp.float32)).astype(
+            jnp.bfloat16
+        )
+    cot_low = jnp.dot(
+        cot_ref[...], back_high_ref[...], preferred_element_type=jnp.float32
+    ) + jnp.dot(cot_ref[...], back_low_ref[...], preferred_element_type=jnp.float32)
+    cot_low = cot_low * scale
+    cot_high = cot_low.astype(jnp.bfloat16)
+    cot_rest = (cot_low - cot_high.astype(jnp.float32)).astype(jnp.bfloat16)
+    for c in range(0, high_ref.shape[0], half):
+        rows = slice(c, c + half)
+        product = (
+            jnp.dot(high_ref[rows, :], cot_high, preferred_element_type=jnp.float32)
+            + jnp.dot(low_ref[rows, :], cot_high, preferred_element_type=jnp.float32)
+            + jnp.dot(high_ref[rows, :], cot_rest, preferred_element_type=jnp.float32)
+        )
+        for n in range(all_ref.shape[0]):
+            all_ref[n, rows, :] = product[:, n * LANES : (n + 1) * LANES]
+    group = lane_index((KEEP, LANES)) // KEEP
+    me = lax.axis_index("tok")
+    for copy in copies:
+        copy.wait()
+    own_lows = to_low([momentum_decay * held_ref[s] for s in range(slots)], split_ref, into_ref)
+    for list_ref, shard, out_ref in ((chosen_ref, me, mine_ref), (other_ref, me ^ 1, theirs_ref)):
+        for h in range(slots // 4):
+            total = jnp.zeros((KEEP, LANES), jnp.float32)
+            for g in range(4):
+                tile = shard * tiles_here + list_ref[4 * h + g]
+                i, j = lax.shift_right_logical(tile, 3), tile & 7
+                block = all_ref[
+                    lax.shift_right_logical(j, 2), pl.ds(pl.multiple_of(i * KEEP, KEEP), KEEP), :
+                ]
+                moved = pltpu.roll(block, (g - (j & 3)) * KEEP & (LANES - 1), 1)
+                total = jnp.where(group == g, moved, total)
+            if out_ref is mine_ref:
+                total = total + own_lows[h]
+            out_ref[h * KEEP : (h + 1) * KEEP, :] = total
+
+
+def own_kernel(
+    chosen_ref, mom_ref, act_ref, cot_ref, sent_ref, near_ref, quad_ref, split_back_ref,
+    back_ref, *rest, scale, spans, tiles_here,
+):
+    sums, (out_ref, grid_ref, tiled_ref, held_ref, sem) = rest[:-5], rest[-5:]
+    copy = pltpu.make_async_copy(mom_ref, held_ref, sem.at[0])
+    copy.start()
+    skip = first_skip(lax.axis_index("tok"), tiles_here, cot_ref.shape[1] // TILE)
     tile_products(
         act_ref, cot_ref, (sent_ref, near_ref), spans * TILE, grid_ref, tiled_ref, scale, spans
     )
-    for copy in copies:
-        copy.wait()
-    places = [
-        pl.ds(pl.multiple_of((skip + chosen_ref[s]) * KEEP, KEEP), KEEP) for s in range(slots)
-    ]
-    picked = [momentum_decay * held_ref[s] + tiled_ref[places[s], :] for s in range(slots)]
-    lows = to_low(picked, split_ref, into_ref)
-    group = lane_index((KEEP, LANES)) // KEEP
     first_half = lax.rem(lane_index((KEEP, 4 * LANES)), LANES) < TILE
-    for h, low in enumerate(lows):
-        low = low + far_low_ref[h * KEEP : (h + 1) * KEEP, :]
-        quad = jnp.where(group + 4 * h < count, low, 0.0).astype(jnp.bfloat16)
-        quad_ref[h * KEEP : (h + 1) * KEEP, :] = quad
-        wide = jnp.dot(
-            quad.astype(jnp.float32), back_ref[...], preferred_element_type=jnp.float32
-        )
+    for h in range(quad_ref.shape[0] // KEEP):
+        quad = quad_ref[h * KEEP : (h + 1) * KEEP, :].astype(jnp.float32)
+        wide = jnp.dot(quad, back_ref[...], preferred_element_type=jnp.float32)
         both = jnp.dot(split_back_ref[...], wide, preferred_element_type=jnp.float32)
         rebuilt = jnp.where(first_half, both[:KEEP, :], both[KEEP:, :])
         for g in range(4):
-            place = places[4 * h + g]
+            at = pl.multiple_of((skip + chosen_ref[4 * h + g]) * KEEP, KEEP)
+            place = pl.ds(at, KEEP)
             tiled_ref[place, :] = tiled_ref[place, :] - rebuilt[:, g * LANES : (g + 1) * LANES]
-    rows = part_ref.shape[0]
-    for c in range(0, rows, 2 * KEEP):
-        part_ref[c : c + 2 * KEEP, :] = tiled_ref[
-            pl.ds(pl.multiple_of(skip * KEEP + c, KEEP), 2 * KEEP), :
-        ].astype(jnp.bfloat16)
+    copy.wait()
+    first = 0
+    for ref in sums:
+        for c in range(0, ref.shape[0], 2 * KEEP):
+            n = min(2 * KEEP, ref.shape[0] - c)
+            rows = slice(first + c, first + c + n)
+            at = pl.ds(pl.multiple_of(skip * KEEP + first + c, KEEP), n)
+            out_ref[rows, :] = (
+                momentum_decay * held_ref[rows, :]
+                + tiled_ref[at, :]
+                + ref[c : c + n, :].astype(jnp.float32)
+            )
+        first += ref.shape[0]
 
 
 def first_row(shard, tiles_here, col_tiles):
@@ -270,64 +320,58 @@
 
 
 def mine_kernel(act_ref, far_ref, near_ref, sems, *, tiles_here, col_tiles):
-    rows = near_ref.shape[0]
-    me = lax.axis_index("tok")
+    me, rows = lax.axis_index("tok"), near_ref.shape[0]
     pick = lambda n: act_ref.at[pl.ds(first_row(me ^ n, tiles_here, col_tiles), rows)]
     run_copies([(pick(2), far_ref), (pick(0), near_ref)], sems)
 
 
-def reorder_kernel(order_ref, from_ref, to_ref, sems):
-    size = from_ref.shape[0]
-    for n in range(size, to_ref.shape[1]):
-        to_ref[:, n] = jnp.zeros_like(to_ref[:, n])
-    run_copies(
-        [
-            (from_ref.at[:, order_ref[n]], to_ref.at[n, pl.ds(0, size)])
-            for n in range(to_ref.shape[0])
-        ],
-        sems,
-    )
-
-
-def finish_kernel(mom_ref, part_ref, *refs):
-    sums, out_ref = refs[:-1], refs[-1]
-    first = 0
-    for ref in sums:
-        for c in range(0, ref.shape[0], 2 * KEEP):
-            n = min(2 * KEEP, ref.shape[0] - c)
-            rows = slice(first + c, first + c + n)
-            out_ref[rows, :] = (
-                momentum_decay * mom_ref[rows, :]
-                + part_ref[rows, :].astype(jnp.float32)
-                + ref[c : c + n, :].astype(jnp.float32)
+def unchanged_kernel(inputs_ref, *refs, tiles_here, list_row):
+    count = len(HELD_ORDER)
+    held, (out_ref, place_ref), rest = refs[:count], refs[count : count + 2], refs[count + 2 :]
+    mine_ref, held_refs, sems = rest[0], rest[1:-1], rest[-1]
+    rep, me = lax.axis_index("replica"), lax.axis_index("tok")
+    used = inputs_ref.shape[0]
+    mine_copies = [
+        pltpu.make_async_copy(
+            inputs_ref.at[:, rep ^ o], mine_ref.at[n, pl.ds(0, used)], sems.at[count + n]
+        )
+        for n, o in enumerate(SHARE_ORDER)
+    ]
+    copies = [
+        pltpu.make_async_copy(a, b, sems.at[n]) for n, (a, b) in enumerate(zip(held, held_refs))
+    ]
+    for n, o in enumerate(SHARE_ORDER):
+        mine_copies[n].start()
+        for copy, k in zip(copies, HELD_ORDER):
+            if k == o:
+                copy.start()
+    for n in range(used, mine_ref.shape[1]):
+        mine_ref[:, n] = jnp.zeros_like(mine_ref[:, n])
+    size = held_refs[0].shape[0]
+    lane = lane_index((1, LANES))
+    total = None
+    for n, o in enumerate(SHARE_ORDER):
+        mine_copies[n].wait()
+        x = mine_ref[n].reshape(size, mine_ref.shape[3])
+        first = 0
+        for copy, k, piece in zip(copies, HELD_ORDER, held_refs):
+            if k != o:
+                continue
+            copy.wait()
+            term = lax.dot_general(
+                x[first : first + piece.shape[0], :], piece[...], (((0,), (0,)), ((), ())),
+                preferred_element_type=jnp.float32,
             )
-        first += ref.shape[0]
-
-
-def unchanged_kernel(mine_ref, *refs, tiles_here, list_row):
-    held, (out_ref, place_ref) = refs[:-2], refs[-2:]
-    size = held[0].shape[0]
-    me = lax.axis_index("tok")
-    lane = lane_index((1, LANES))
-    slots_at = [(o, [r for r, k in zip(held, HELD_ORDER) if k == o]) for o in SHARE_ORDER]
-    total = None
-    for n, (_, pieces) in enumerate(slots_at):
-        first = n * size
-        for piece in pieces:
-            x = mine_ref[first : first + piece.shape[0], :]
             first += piece.shape[0]
-            term = lax.dot_general(
-                x, piece[...], (((0,), (0,)), ((), ())), preferred_element_type=jnp.float32
-            )
             total = term if total is None else total + term
-        piece = pieces[-1]
-        at = list_row - (size - piece.shape[0])
-        lists = piece[at : at + 8, :LANES].astype(jnp.float32).astype(jnp.int32)
+            last = piece
+        at = list_row - (size - last.shape[0])
+        lists = last[at : at + 8, :LANES].astype(jnp.float32).astype(jnp.int32)
         row = jnp.zeros((1, LANES), jnp.int32)
         for d, offset in enumerate(TOK_ORDER):
             tile = lists[d : d + 1, :] + (me ^ offset) * tiles_here
             i, j = lax.shift_right_logical(tile, 3), tile & 7
-            packed = (lax.shift_right_logical(j, 2) * place_rows(mine_ref) + i * KEEP) * LANES
+            packed = (lax.shift_right_logical(j, 2) * place_rows(used) + i * KEEP) * LANES
             packed = packed + (j & 3) * KEEP
             packed = pltpu.roll(packed, 8 * d, 1)
             row = jnp.where((lane >= 8 * d) & (lane < 8 * (d + 1)), packed, row)
@@ -335,9 +379,8 @@
     out_ref[...] = total
 
 
-def place_rows(mine_ref):
-    depth = mine_ref.shape[0] - 8 * len(SHARE_ORDER)
-    return -(-(depth // TILE * KEEP) // LANES) * LANES
+def place_rows(row_tiles):
+    return -(-(row_tiles * KEEP) // LANES) * LANES
 
 
 def lows_kernel(inputs_ref, high_ref, low_ref, out_ref, lows_ref, *, span):
@@ -374,17 +417,10 @@
     lax.fori_loop(0, quads_ref.shape[0], add_list, 0)
 
 
-def begin_kernel(place_ref, *refs, at):
-    quads, sum_ref = refs[:-1], refs[-1]
+def last_kernel(place_ref, lows_ref, base_ref, across_ref, *refs):
+    quads, (out_ref, sum_ref) = refs[:-2], refs[-2:]
     sum_ref[...] = jnp.zeros_like(sum_ref)
-    for n, ref in zip(at, quads):
-        add_quads(place_ref, n, ref, sum_ref)
-
-
-def last_kernel(place_ref, lows_ref, base_ref, across_ref, begun_ref, *refs, at):
-    quads, (out_ref, sum_ref) = refs[:-2], refs[-2:]
-    sum_ref[...] = begun_ref[...]
-    for n, ref in zip(at, quads):
+    for n, ref in enumerate(quads):
         add_quads(place_ref, n, ref, sum_ref)
     rows = lows_ref.shape[1]
     whole = jnp.concatenate(
@@ -484,26 +520,6 @@
         return (offset & 1) * 2 + lax.shift_right_logical(offset, 1)
 
     anywhere = pl.BlockSpec(memory_space=pltpu.HBM)
-    span_shape = jax.ShapeDtypeStruct((span_rows, tokens), jnp.bfloat16)
-    sent_rows, near_rows = pl.pallas_call(
-        functools.partial(prepare_kernel, tiles_here=tiles_here),
-        out_shape=[
-            jax.ShapeDtypeStruct((span_rows + width, tokens), jnp.bfloat16), span_shape,
-        ],
-        in_specs=[anywhere] * 2,
-        out_specs=vmem(2),
-        scratch_shapes=[pltpu.SemaphoreType.DMA((2 + width // tokens,))],
-        name="prepare",
-    )(act, cotangent)
-    sent_far = swap(sent_rows, "tok", 1)
-    mine_far, mine_near = pl.pallas_call(
-        functools.partial(mine_kernel, tiles_here=tiles_here, col_tiles=col_tiles),
-        out_shape=[span_shape] * 2,
-        in_specs=[anywhere],
-        out_specs=vmem(2),
-        scratch_shapes=[pltpu.SemaphoreType.DMA((2,))],
-        name="mine",
-    )(act)
     share = TILE * TILE // replicas
     listed = chosen[0, 0].astype(jnp.bfloat16)
     pad_rows = -(tiles_here + 1) % 8 + 1
@@ -516,52 +532,94 @@
     )[None]
     piece_far = swap(piece, "tok", 2)
     pair = jnp.concatenate([piece, piece_far], axis=0)
-    pieces = jnp.concatenate([pair, swap(pair, "tok", 1)], axis=0)
+    pair_near = swap(pair, "tok", 1)
+    sent_rows, near_rows = pl.pallas_call(
+        functools.partial(prepare_kernel, tiles_here=tiles_here),
+        out_shape=[
+            jax.ShapeDtypeStruct((span_rows + width, tokens), jnp.bfloat16),
+            jax.ShapeDtypeStruct((span_rows, tokens), jnp.bfloat16),
+        ],
+        in_specs=[anywhere] * 2,
+        out_specs=vmem(2),
+        scratch_shapes=[pltpu.SemaphoreType.DMA((2 + width // tokens,))],
+        name="prepare",
+    )(act, cotangent)
+    sent_far = swap(sent_rows, "tok", 1)
+    mine_far, mine_near = pl.pallas_call(
+        functools.partial(mine_kernel, tiles_here=tiles_here, col_tiles=col_tiles),
+        out_shape=[jax.ShapeDtypeStruct((span_rows, tokens), jnp.bfloat16)] * 2,
+        in_specs=[anywhere],
+        out_specs=vmem(2),
+        scratch_shapes=[pltpu.SemaphoreType.DMA((2,))],
+        name="mine",
+    )(act)
+    far_chosen = piece_far[0, tiles_here, :slots].astype(jnp.int32)
+    near_chosen = pair_near[0, tiles_here, :slots].astype(jnp.int32)
+    pieces = jnp.concatenate([pair, pair_near], axis=0)
     sent_near = swap(near_rows, "tok", 1)
-    far_chosen = piece_far[0, tiles_here, :slots].astype(jnp.int32)
+
+    moment = momentum.reshape(tiles_here * KEEP, LANES)
+    low = low_rows().astype(np.float32)
+    at_once = 5
+    sum_rows = place_rows(row_tiles)
+    along_high, along_low = split_bf16(np.kron(np.eye(at_once, dtype=np.float32), low))
+    across = np.kron(np.eye(col_tiles, dtype=np.float32), low)
+    low_shape = jax.ShapeDtypeStruct((slots // 4 * KEEP, LANES), jnp.float32)
+    low_mine, low_near = pl.pallas_call(
+        functools.partial(factor_lows_kernel, scale=scale, tiles_here=tiles_here),
+        out_shape=[low_shape] * 2,
+        in_specs=smem(2) + [anywhere] + vmem(8),
+        out_specs=vmem(2),
+        scratch_shapes=[pltpu.VMEM((row_tiles * KEEP, tokens), jnp.bfloat16)] * 2
+        + [
+            pltpu.VMEM((col_tiles // 4, row_tiles * KEEP, LANES), jnp.float32),
+            pltpu.VMEM((slots, KEEP, LANES), jnp.float32),
+            pltpu.SemaphoreType.DMA((slots,)),
+        ],
+        name="factor_lows",
+    )(
+        chosen[0, 0], near_chosen, moment, act, cotangent, along_high, along_low,
+        *split_bf16(np.ascontiguousarray(across.T)), split, into,
+    )
+    low_from_near = swap(low_near, "tok", 1)
+
     grid_scratch = [
         pltpu.VMEM((width // LANES, 2 * TILE, LANES), jnp.float32),
         pltpu.VMEM((spans * col_tiles * KEEP, LANES), jnp.float32),
     ]
-    cuts = [tiles_here * 8 // 15, tiles_here // 9]
+    cuts = [tiles_here * 2 // 15, tiles_here // 5]
     cuts.append(tiles_here - sum(cuts))
     far_low, *far_sums = pl.pallas_call(
         functools.partial(far_kernel, scale=scale, spans=spans, tiles_here=tiles_here),
-        out_shape=[jax.ShapeDtypeStruct((slots // 4 * KEEP, LANES), jnp.float32)]
+        out_shape=[low_shape]
         + [jax.ShapeDtypeStruct((n * KEEP, LANES), jnp.bfloat16) for n in cuts],
         in_specs=smem(1) + vmem(5),
         out_specs=vmem(1 + len(cuts)),
         scratch_shapes=grid_scratch,
+        compiler_params=room(12),
         name="far",
     )(far_chosen, mine_far, cotangent, sent_far, split, into)
-    low_from = swap(far_low, "tok", 2)
+    low_from_far = swap(far_low, "tok", 2)
     sums_from = []
     for part in far_sums:
         sums_from.append(swap(part, "tok", 2))
 
-    moment = momentum.reshape(tiles_here * KEEP, LANES)
-    own_part, quads = pl.pallas_call(
+    at = np.arange(low_shape.shape[0])[:, None] // KEEP * 4 + np.arange(LANES) // KEEP
+    quads = jnp.where(
+        jnp.asarray(at, jnp.int32) < counts[0, 0], low_mine + low_from_near + low_from_far, 0.0
+    ).astype(jnp.bfloat16)
+    new_momentum = pl.pallas_call(
         functools.partial(own_kernel, scale=scale, spans=spans, tiles_here=tiles_here),
-        out_shape=(
-            jax.ShapeDtypeStruct((tiles_here * KEEP, LANES), jnp.bfloat16),
-            jax.ShapeDtypeStruct((slots // 4 * KEEP, LANES), jnp.bfloat16),
-        ),
-        in_specs=smem(2) + vmem(4) + [anywhere] + vmem(5),
-        out_specs=tuple(vmem(2)),
+        out_shape=jax.ShapeDtypeStruct(moment.shape, jnp.float32),
+        in_specs=smem(1) + [anywhere] + vmem(7 + len(cuts)),
+        out_specs=vmem(1)[0],
         scratch_shapes=grid_scratch
-        + [pltpu.VMEM((slots, KEEP, LANES), jnp.float32), pltpu.SemaphoreType.DMA((slots,))],
+        + [pltpu.VMEM(moment.shape, jnp.float32), pltpu.SemaphoreType.DMA((1,))],
         name="own",
     )(
-        counts[0], chosen[0, 0], mine_near, cotangent, sent_far, sent_near, moment, low_from,
-        split, into, split_back, back,
-    )
-    new_momentum = pl.pallas_call(
-        finish_kernel,
-        out_shape=jax.ShapeDtypeStruct(moment.shape, jnp.float32),
-        in_specs=vmem(2 + len(cuts)),
-        out_specs=vmem(1)[0],
-        name="finish",
-    )(moment, own_part, *sums_from).reshape(momentum.shape)
+        chosen[0, 0], moment, mine_near, cotangent, sent_far, sent_near, quads, split_back,
+        back, *sums_from,
+    ).reshape(momentum.shape)
 
     whole = jnp.concatenate(
         [
@@ -576,24 +634,14 @@
     list_rows = jnp.zeros((8, width), jnp.bfloat16)
     list_rows = list_rows.at[:shards, :slots].set(pieces[:, tiles_here, :slots])
     held = {0: jnp.concatenate([matrix, list_rows], axis=0)}
-    cut = held[0].shape[0] // 2
     held[2] = swap(held[0], "replica", 2)
     held[4] = swap(held[0], "replica", 4)
-    six = [swap(held[2][:cut], "replica", 4)]
-    six.append(swap(held[4][cut:], "replica", 2))
-    near = [held[0], held[2], held[4], *six]
-    held_all = near + [swap(h, "replica", 1) for h in near]
+    held[6] = swap(held[2], "replica", 4)
+    near = [held[o] for o in (0, 2, 4, 6)]
+    held_all = list(near)
+    for h in near:
+        held_all.append(swap(h, "replica", 1))
     by_share = inputs.reshape(row_tiles, replicas, rows_share, tokens)
-    mine = pl.pallas_call(
-        reorder_kernel,
-        out_shape=jax.ShapeDtypeStruct(
-            (replicas, held[0].shape[0] // rows_share, rows_share, tokens), jnp.bfloat16
-        ),
-        in_specs=smem(1) + [anywhere],
-        out_specs=vmem(1)[0],
-        scratch_shapes=[pltpu.SemaphoreType.DMA((replicas,))],
-        name="reorder",
-    )(rep ^ jnp.asarray(SHARE_ORDER, jnp.int32), by_share)
     unchanged, places = pl.pallas_call(
         functools.partial(
             unchanged_kernel, tiles_here=tiles_here, list_row=matrix.shape[0]
@@ -602,16 +650,16 @@
             jax.ShapeDtypeStruct((tokens, width), jnp.float32),
             jax.ShapeDtypeStruct((replicas, LANES), jnp.int32),
         ],
-        in_specs=vmem(1 + len(held_all)),
+        in_specs=[anywhere] * (1 + len(held_all)),
         out_specs=vmem(2),
+        scratch_shapes=[
+            pltpu.VMEM((replicas, held[0].shape[0] // rows_share, rows_share, tokens), jnp.bfloat16)
+        ]
+        + [pltpu.VMEM(h.shape, jnp.bfloat16) for h in held_all]
+        + [pltpu.SemaphoreType.DMA((replicas + len(held_all),))],
         name="unchanged",
-    )(mine.reshape(-1, tokens), *held_all)
-
-    low = low_rows().astype(np.float32)
-    at_once = 5
-    sum_rows = -(-row_tiles * KEEP // LANES) * LANES
-    along = np.kron(np.eye(at_once, dtype=np.float32), low)
-    along_high, along_low = split_bf16(along)
+    )(by_share, *held_all)
+
     lows = pl.pallas_call(
         functools.partial(lows_kernel, span=at_once * TILE),
         out_shape=jax.ShapeDtypeStruct((tokens, sum_rows), jnp.bfloat16),
@@ -629,25 +677,15 @@
     brought[6] = swap(brought[2], "replica", 4)
     for o in (0, 2, 4, 6):
         brought[o ^ 1] = swap(brought[o], "replica", 1)
-    early = len(SHARE_ORDER) - 2
-    begun = pl.pallas_call(
-        functools.partial(begin_kernel, at=range(early)),
-        out_shape=jax.ShapeDtypeStruct((col_tiles // 4 * sum_rows, LANES), jnp.float32),
-        in_specs=smem(1) + vmem(early),
+    values = pl.pallas_call(
+        last_kernel,
+        out_shape=jax.ShapeDtypeStruct((tokens, width), jnp.bfloat16),
+        in_specs=smem(1) + vmem(3 + len(SHARE_ORDER)),
         out_specs=vmem(1)[0],
-        compiler_params=room(12),
-        name="begin",
-    )(places, *[brought[o] for o in SHARE_ORDER[:early]])
-    across = np.kron(np.eye(col_tiles, dtype=np.float32), low).astype(jnp.bfloat16)
-    values = pl.pallas_call(
-        functools.partial(last_kernel, at=range(early, len(SHARE_ORDER))),
-        out_shape=jax.ShapeDtypeStruct((tokens, width), jnp.bfloat16),
-        in_specs=smem(1) + vmem(4 + len(SHARE_ORDER) - early),
-        out_specs=vmem(1)[0],
-        scratch_shapes=[pltpu.VMEM(begun.shape, jnp.float32)],
+        scratch_shapes=[pltpu.VMEM((col_tiles // 4 * sum_rows, LANES), jnp.float32)],
         compiler_params=room(12),
         name="last",
-    )(places, lows, unchanged, across, begun, *[brought[o] for o in SHARE_ORDER[early:]])
+    )(places, lows, unchanged, across.astype(jnp.bfloat16), *[brought[o] for o in SHARE_ORDER])
     return (values, new_momentum)
 
 

time: 114 us -> 119 us (1.044)
  waiting for transfers between devices: 39.4 us -> 57 us
  starting transfers between devices: 31.6 us -> 27.6 us
  Pallas kernels: 31.4 us -> 28 us
  local copies, waits for them, and re-layouts: 6.02 us -> 3.21 us
  other arithmetic: 3.37 us -> 1.53 us
    ppermute x26 -> x25, waiting for transfers between devices: 39.4 us -> 57 us  [swap(): return lax.ppermute(array, axis, [(i, i ^ bit) for i in range(size)])]
    ppermute x26 -> x25, starting transfers between devices: 31.6 us -> 27.6 us  [swap(): return lax.ppermute(array, axis, [(i, i ^ bit) for i in range(size)])]
    unnamed x41 -> x43, local copies, waits for them, and re-layouts: 4.99 us -> 2.21 us
    pallas_call x4 -> x2, Pallas kernels: 12.1 us -> 9.66 us  [the longest x1 4.87 us: four_shards(): pl.pallas_call(last_kernel, out_shape=jax.ShapeDtypeStruct((tokens, width...]
    pallas_call x1, Pallas kernels: 3.06 us -> 1.68 us  [four_shards(): pl.pallas_call(functools.partial(far_kernel, scale=scale, spans=spans, ti...]
  transfers between devices with their start and end apart: 26 -> 25, of which waited for: 10 -> 10; matrix products, arithmetic and copies ran while one was open for 3% -> 1% of each run, Pallas kernels for 25% -> 19%
where the time goes in v1:
time: 119 us
  waiting for transfers between devices  57 us (48%)
  Pallas kernels  28 us (24%)
  starting transfers between devices  27.6 us (23%)
  local copies, waits for them, and re-layouts  3.21 us (3%)
  between operations  1.67 us (1%)
  other arithmetic  1.53 us (1%)
    ppermute x25, waiting for transfers between devices, swap(): return lax.ppermute(array, axis, [(i, i ^ bit) for i in range(size)])  57 us
    ppermute x25, starting transfers between devices, swap(): return lax.ppermute(array, axis, [(i, i ^ bit) for i in range(size)])  27.6 us
    pallas_call x1, Pallas kernels, four_shards(): pl.pallas_call(functools.partial(own_kernel, scale=scale, spans=spans, ti...  5.11 us
    pallas_call x1, Pallas kernels, four_shards(): pl.pallas_call(last_kernel, out_shape=jax.ShapeDtypeStruct((tokens, width...  4.87 us
    pallas_call x1, Pallas kernels, four_shards(): pl.pallas_call(functools.partial(factor_lows_kernel, scale=scale, tiles_h...  4.79 us
    pallas_call x1, Pallas kernels, four_shards(): pl.pallas_call(functools.partial(unchanged_kernel, tiles_here=tiles_here,...  4.04 us
    pallas_call x1, Pallas kernels, four_shards(): pl.pallas_call(functools.partial(lows_kernel, span=at_once * TILE), out_s...  3.34 us
  transfers between devices with their start and end apart: 25, of which 10 were waited for; matrix products, arithmetic and copies ran while one was open for 1% of the time, Pallas kernels for 19%

profile of v1, /device:TPU:0, one launch (start us, length us, event | category | flops | bytes accessed | tf_op | source)
XLA Modules:
  0.0 119.0 jit_solution(9245216308568197822)
XLA Ops:
  0.6 0.0 copy-start
  0.7 0.7 convert_bitcast_fusion
  1.4 0.4 copy-done
  1.8 4.1 %collective-permute-start = (bf16[1,96,512]{2,1,0:T(8,128)(2,1)S(1)}, bf16[1,96,512]{2,1,0:T(8,128)(2,1)S(1)}, u32[]{:S(2)}, u32[]{:S(2)}) collective-permute-start(bf16[1,96,512]{2,1,0:T(8,128)(2,1)S(1)} %fusion.4), channel_id=1, source_target_pairs={{0,2},{1,3},{2,0},{3,1},{4,6},{5,7},{6,4},{7,5},{8,10},{9,11},{10,... | collective-permute-start | bytes 294920 | tf_op jit(solution)/shard_map/ppermute | solution.py:459
  5.9 4.9 %collective-permute-done = bf16[1,96,512]{2,1,0:T(8,128)(2,1)S(1)} collective-permute-done((bf16[1,96,512]{2,1,0:T(8,128)(2,1)S(1)}, bf16[1,96,512]{2,1,0:T(8,128)(2,1)S(1)}, u32[]{:S(2)}, u32[]{:S(2)}) %collective-permute-start) | collective-permute-done | bytes 98336 | tf_op jit(solution)/shard_map/ppermute | solution.py:459
  10.9 0.8 collective-permute-start.1
  11.6 2.2 %prepare.1 = (bf16[1280,256]{1,0:T(8,128)(2,1)}, bf16[768,256]{1,0:T(8,128)(2,1)}) custom-call(bf16[2880,256]{1,0:T(8,128)(2,1)} %bitcast.40, bf16[256,512]{1,0:T(8,128)(2,1)} %cot_ref.7), custom_call_target="tpu_custom_call" | custom-call | tf_op jit(solution)/shard_map/prepare/pallas_call | solution.py:536
  13.8 1.4 %collective-permute-start.21 = (bf16[768,256]{1,0:T(8,128)(2,1)}, bf16[768,256]{1,0:T(8,128)(2,1)}, u32[]{:S(2)}, u32[]{:S(2)}) collective-permute-start(bf16[768,256]{1,0:T(8,128)(2,1)} %get-tuple-element.46), channel_id=1, source_target_pairs={{0,1},{1,0},{2,3},{3,2},{4,5},{5,4},{6,7},{7,6},{8,9},{9,8},{10,11... | collective-permute-start | bytes 1179656 | tf_op jit(solution)/shard_map/ppermute | solution.py:459
  15.2 0.7 collective-permute-start.10
  15.9 2.0 %mine.1 = (bf16[768,256]{1,0:T(8,128)(2,1)}, bf16[768,256]{1,0:T(8,128)(2,1)}) custom-call(bf16[2880,256]{1,0:T(8,128)(2,1)} %bitcast.41), custom_call_target="tpu_custom_call" | custom-call | tf_op jit(solution)/shard_map/mine/pallas_call | solution.py:548
  18.0 0.0 collective-permute-done.1
  18.1 0.1 pad_maximum_fusion.1
  18.2 0.4 reshape.93
  18.6 0.1 copy.26
  18.7 0.4 reshape.94
  19.2 1.6 %collective-permute-start.2 = (bf16[368,512]{1,0:T(8,128)(2,1)S(1)}, bf16[368,512]{1,0:T(8,128)(2,1)}, u32[]{:S(2)}, u32[]{:S(2)}) collective-permute-start(bf16[368,512]{1,0:T(8,128)(2,1)S(1)} %fusion.1.refs_0_), channel_id=1, source_target_pairs={{0,8},{4,12},{8,0},{12,4},{16,24},{20,28},{24,16},{28,20},{1,9},{5... | collective-permute-start | bytes 1130504 | tf_op jit(solution)/shard_map/ppermute | solution.py:459
  20.8 0.6 fusion.6.other_ref
  21.4 4.8 %factor_lows.1 = (f32[64,128]{1,0:T(8,128)}, f32[64,128]{1,0:T(8,128)}) custom-call(s32[8]{0:T(128)} %bitcast.53, s32[8]{0:T(128)} %fusion.6.other_ref, f32[2880,128]{1,0:T(8,128)} %bitcast.45, bf16[2880,256]{1,0:T(8,128)(2,1)} %bitcast.42, bf16[256,512]{1,0:T(8,128)(2,1)} %cot_ref.7, bf16[160,320]{1,0:T(8,128)(2,1)} %constant.103.clone.high_ref.along_high_ref, ...), custom_call_target="tpu_custom_call" | custom-call | tf_op jit(solution)/shard_map/factor_lows/pallas_call | solution.py:568
  26.1 0.0 copy-start.19
  26.2 0.0 copy-start.20
  26.2 1.5 %collective-permute-start.9 = (f32[64,128]{1,0:T(8,128)}, f32[64,128]{1,0:T(8,128)S(1)}, u32[]{:S(2)}, u32[]{:S(2)}) collective-permute-start(f32[64,128]{1,0:T(8,128)} %get-tuple-element.41), channel_id=1, source_target_pairs={{0,1},{1,0},{2,3},{3,2},{4,5},{5,4},{6,7},{7,6},{8,9},{9,8},{10,11... | collective-permute-start | bytes 98312 | tf_op jit(solution)/shard_map/ppermute | solution.py:459
  27.7 12.1 %collective-permute-done.10.sent_ref = bf16[1280,256]{1,0:T(8,128)(2,1)S(1)} collective-permute-done((bf16[1280,256]{1,0:T(8,128)(2,1)}, bf16[1280,256]{1,0:T(8,128)(2,1)S(1)}, u32[]{:S(2)}, u32[]{:S(2)}) %collective-permute-start.10) | collective-permute-done | bytes 655392 | tf_op jit(solution)/shard_map/ppermute | solution.py:459
  39.8 1.7 %far.1 = (f32[64,128]{1,0:T(8,128)S(1)}, bf16[384,128]{1,0:T(8,128)(2,1)S(1)}, bf16[576,128]{1,0:T(8,128)(2,1)S(1)}, bf16[1920,128]{1,0:T(8,128)(2,1)S(1)}) custom-call(s32[8]{0:T(128)S(1)} %fusion.5.chosen_ref, bf16[768,256]{1,0:T(8,128)(2,1)S(1)} %copy-done.6, bf16[256,512]{1,0:T(8,128)(2,1)S(1)} %copy-done.1, ...), custom_call_target="tpu_custom_call" | custom-call | tf_op jit(solution)/shard_map/far/pallas_call | solution.py:592
  41.5 3.2 %collective-permute-start.11 = (f32[64,128]{1,0:T(8,128)S(1)}, f32[64,128]{1,0:T(8,128)S(1)}, u32[]{:S(2)}, u32[]{:S(2)}) collective-permute-start(f32[64,128]{1,0:T(8,128)S(1)} %get-tuple-element.44), channel_id=1, source_target_pairs={{0,2},{1,3},{2,0},{3,1},{4,6},{5,7},{6,4},{7,5},{8,10},{9,11},{10,... | collective-permute-start | bytes 98312 | tf_op jit(solution)/shard_map/ppermute | solution.py:459
  45.4 0.1 collective-permute-start.5
  45.4 0.0 collective-permute-done.9
  45.5 1.6 %collective-permute-start.3 = (bf16[368,512]{1,0:T(8,128)(2,1)S(1)}, bf16[368,512]{1,0:T(8,128)(2,1)S(1)}, u32[]{:S(2)}, u32[]{:S(2)}) collective-permute-start(bf16[368,512]{1,0:T(8,128)(2,1)S(1)} %fusion.1.refs_0_), channel_id=1, source_target_pairs={{0,16},{4,20},{8,24},{12,28},{16,0},{20,4},{24,8},{28,12},{1,17},{... | collective-permute-start | bytes 1130504 | tf_op jit(solution)/shard_map/ppermute | solution.py:459
  47.0 0.0 collective-permute-done.2.refs_1_
  47.1 0.5 collective-permute-start.4
  47.6 0.0 collective-permute-done.11
  47.6 2.0 %collective-permute-start.12 = (bf16[1,64,128]{2,1,0:T(8,128)(2,1)S(1)}, bf16[1,64,128]{2,1,0:T(8,128)(2,1)S(1)}, u32[]{:S(2)}, u32[]{:S(2)}) collective-permute-start(bf16[1,64,128]{2,1,0:T(8,128)(2,1)S(1)} %bitcast.49), channel_id=1, source_target_pairs={{0,2},{1,3},{2,0},{3,1},{4,6},{5,7},{6,4},{7,5},{8,10},{9,11},{10,... | collective-permute-start | bytes 49160 | tf_op jit(solution)/shard_map/ppermute | solution.py:459
  49.6 2.9 %collective-permute-done.12 = bf16[1,64,128]{2,1,0:T(8,128)(2,1)S(1)} collective-permute-done((bf16[1,64,128]{2,1,0:T(8,128)(2,1)S(1)}, bf16[1,64,128]{2,1,0:T(8,128)(2,1)S(1)}, u32[]{:S(2)}, u32[]{:S(2)}) %collective-permute-start.12) | collective-permute-done | bytes 16416 | tf_op jit(solution)/shard_map/ppermute | solution.py:459
  52.5 1.8 %collective-permute-start.24 = (bf16[1920,128]{1,0:T(8,128)(2,1)S(1)}, bf16[1920,128]{1,0:T(8,128)(2,1)S(1)}, u32[]{:S(2)}, u32[]{:S(2)}) collective-permute-start(bf16[1920,128]{1,0:T(8,128)(2,1)S(1)} %get-tuple-element.49), channel_id=1, source_target_pairs={{0,2},{1,3},{2,0},{3,1},{4,6},{5,7},{6,4},{7,5},{8,10},{9,11},{10,... | collective-permute-start | bytes 1474568 | tf_op jit(solution)/shard_map/ppermute | solution.py:459
  54.3 0.0 collective-permute-done.21.near_ref
  54.3 1.9 %collective-permute-start.13 = (bf16[2,64,128]{2,1,0:T(8,128)(2,1)S(1)}, bf16[2,64,128]{2,1,0:T(8,128)(2,1)S(1)}, u32[]{:S(2)}, u32[]{:S(2)}) collective-permute-start(bf16[2,64,128]{2,1,0:T(8,128)(2,1)S(1)} %pad_maximum_fusion.4), channel_id=1, source_target_pairs={{0,1},{1,0},{2,3},{3,2},{4,5},{5,4},{6,7},{7,6},{8,9},{9,8},{10,11... | collective-permute-start | bytes 98312 | tf_op jit(solution)/shard_map/ppermute | solution.py:459
  56.2 0.9 collective-permute-start.22
  57.1 0.1 collective-permute-done.3.refs_2_
  57.2 6.6 %collective-permute-done.13 = bf16[2,64,128]{2,1,0:T(8,128)(2,1)S(1)} collective-permute-done((bf16[2,64,128]{2,1,0:T(8,128)(2,1)S(1)}, bf16[2,64,128]{2,1,0:T(8,128)(2,1)S(1)}, u32[]{:S(2)}, u32[]{:S(2)}) %collective-permute-start.13) | collective-permute-done | bytes 32800 | tf_op jit(solution)/shard_map/ppermute | solution.py:459
  63.7 0.0 collective-permute-start.7
  63.8 16.0 %collective-permute-done.22.rest_0_ = bf16[384,128]{1,0:T(8,128)(2,1)S(1)} collective-permute-done((bf16[384,128]{1,0:T(8,128)(2,1)S(1)}, bf16[384,128]{1,0:T(8,128)(2,1)S(1)}, u32[]{:S(2)}, u32[]{:S(2)}) %collective-permute-start.22) | collective-permute-done | bytes 98336 | tf_op jit(solution)/shard_map/ppermute | solution.py:459
  79.8 1.5 %collective-permute-start.15 = (bf16[4,64,128]{2,1,0:T(8,128)(2,1)S(1)}, bf16[4,64,128]{2,1,0:T(8,128)(2,1)S(1)}, u32[]{:S(2)}, u32[]{:S(2)}) collective-permute-start(bf16[4,64,128]{2,1,0:T(8,128)(2,1)S(1)} %pad_maximum_fusion.3.refs_0_), channel_id=1, source_target_pairs={{0,16},{4,20},{8,24},{12,28},{16,0},{20,4},{24,8},{28,12},{1,17},{... | collective-permute-start | bytes 196616 | tf_op jit(solution)/shard_map/ppermute | solution.py:459
  81.3 0.0 collective-permute-done.4.refs_3_
  81.3 2.7 %collective-permute-done.15.refs_2_ = bf16[4,64,128]{2,1,0:T(8,128)(2,1)S(1)} collective-permute-done((bf16[4,64,128]{2,1,0:T(8,128)(2,1)S(1)}, bf16[4,64,128]{2,1,0:T(8,128)(2,1)S(1)}, u32[]{:S(2)}, u32[]{:S(2)}) %collective-permute-start.15) | collective-permute-done | bytes 65568 | tf_op jit(solution)/shard_map/ppermute | solution.py:459
  84.1 1.5 %collective-permute-start.14 = (bf16[4,64,128]{2,1,0:T(8,128)(2,1)S(1)}, bf16[4,64,128]{2,1,0:T(8,128)(2,1)S(1)}, u32[]{:S(2)}, u32[]{:S(2)}) collective-permute-start(bf16[4,64,128]{2,1,0:T(8,128)(2,1)S(1)} %pad_maximum_fusion.3.refs_0_), channel_id=1, source_target_pairs={{0,8},{4,12},{8,0},{12,4},{16,24},{20,28},{24,16},{28,20},{1,9},{5... | collective-permute-start | bytes 196616 | tf_op jit(solution)/shard_map/ppermute | solution.py:459
  85.5 2.8 %collective-permute-done.14.refs_1_ = bf16[4,64,128]{2,1,0:T(8,128)(2,1)S(1)} collective-permute-done((bf16[4,64,128]{2,1,0:T(8,128)(2,1)S(1)}, bf16[4,64,128]{2,1,0:T(8,128)(2,1)S(1)}, u32[]{:S(2)}, u32[]{:S(2)}) %collective-permute-start.14) | collective-permute-done | bytes 65568 | tf_op jit(solution)/shard_map/ppermute | solution.py:459
  88.3 6.1 %collective-permute-done.23.rest_1_ = bf16[576,128]{1,0:T(8,128)(2,1)S(1)} collective-permute-done((bf16[576,128]{1,0:T(8,128)(2,1)S(1)}, bf16[576,128]{1,0:T(8,128)(2,1)S(1)}, u32[]{:S(2)}, u32[]{:S(2)}) %collective-permute-start.23) | collective-permute-done | bytes 147488 | tf_op jit(solution)/shard_map/ppermute | solution.py:459
  94.4 1.5 %collective-permute-start.19 = (bf16[4,64,128]{2,1,0:T(8,128)(2,1)S(1)}, bf16[4,64,128]{2,1,0:T(8,128)(2,1)S(1)}, u32[]{:S(2)}, u32[]{:S(2)}) collective-permute-start(bf16[4,64,128]{2,1,0:T(8,128)(2,1)S(1)} %collective-permute-done.14.refs_1_), channel_id=1, source_target_pairs={{0,16},{4,20},{8,24},{12,28},{16,0},{20,4},{24,8},{28,12},{1,17},{... | collective-permute-start | bytes 196616 | tf_op jit(solution)/shard_map/ppermute | solution.py:459
  95.9 2.7 %collective-permute-done.19.refs_6_ = bf16[4,64,128]{2,1,0:T(8,128)(2,1)S(1)} collective-permute-done((bf16[4,64,128]{2,1,0:T(8,128)(2,1)S(1)}, bf16[4,64,128]{2,1,0:T(8,128)(2,1)S(1)}, u32[]{:S(2)}, u32[]{:S(2)}) %collective-permute-start.19) | collective-permute-done | bytes 65568 | tf_op jit(solution)/shard_map/ppermute | solution.py:459
  98.7 0.0 collective-permute-done.7.refs_6_
  98.7 0.5 collective-permute-start.17
  99.2 0.1 collective-permute-start.18
  99.3 0.0 collective-permute-done.24.rest_2_
  99.3 0.5 collective-permute-start.20
  99.8 3.3 %lows.1.lows_ref = bf16[256,1536]{1,0:T(8,128)(2,1)} custom-call(bf16[2880,256]{1,0:T(8,128)(2,1)} %bitcast.43, bf16[160,320]{1,0:T(8,128)(2,1)} %constant.103.clone.high_ref.along_high_ref, bf16[160,320]{1,0:T(8,128)(2,1)} %constant.104.clone.low_ref.along_low_ref), custom_call_target="tpu_custom_call" | custom-call | tf_op jit(solution)/shard_map/lows/pallas_call | solution.py:663
  103.1 5.1 %own.1 = f32[2880,128]{1,0:T(8,128)} custom-call(s32[8]{0:T(128)} %bitcast.54, f32[2880,128]{1,0:T(8,128)} %bitcast.46, bf16[768,256]{1,0:T(8,128)(2,1)} %get-tuple-element.45.act_ref, bf16[256,512]{1,0:T(8,128)(2,1)} %cot_ref.7, bf16[1280,256]{1,0:T(8,128)(2,1)} %copy-done.3, bf16[768,256]{1,0:T(8,128)(2,1)} %collective-permute-done.21.near_ref, ...), custom_call_target="tpu_custom_call" | custom-call | tf_op jit(solution)/shard_map/own/pallas_call | solution.py:611
  108.3 0.0 collective-permute-done.8.refs_7_
  108.3 0.0 copy-start.7
  108.3 4.0 %unchanged.1 = (f32[256,512]{1,0:T(8,128)}, s32[8,128]{1,0:T(8,128)}) custom-call(bf16[45,8,8,256]{3,2,1,0:T(8,128)(2,1)} %bitcast.44, bf16[368,512]{1,0:T(8,128)(2,1)} %copy-done.10, bf16[368,512]{1,0:T(8,128)(2,1)} %collective-permute-done.2.refs_1_, bf16[368,512]{1,0:T(8,128)(2,1)} %copy-done.13, bf16[368,512]{1,0:T(8,128)(2,1)} %collective-permute-done.4.refs_3_, ...), custom_call_target="tpu_custom_call" | custom-call | tf_op jit(solution)/shard_map/unchanged/pallas_call | solution.py:645
  112.3 0.0 collective-permute-done.16.refs_3_
  112.4 0.0 collective-permute-done.18.refs_5_
  112.4 0.0 collective-permute-done.20.refs_7_
  112.4 1.0 copy-done.5
  113.4 0.7 copy-done.9
  114.1 4.9 %last.1 = bf16[256,512]{1,0:T(8,128)(2,1)} custom-call(s32[8,128]{1,0:T(8,128)S(1)} %copy-done.9, bf16[256,1536]{1,0:T(8,128)(2,1)S(1)} %copy-done.2, f32[256,512]{1,0:T(8,128)S(1)} %copy-done.5, bf16[256,512]{1,0:T(8,128)(2,1)S(1)} %copy-done.7, bf16[4,64,128]{2,1,0:T(8,128)(2,1)S(1)} %pad_maximum_fusion.3.refs_0_, ...), custom_call_target="tpu_custom_call" | custom-call | tf_op jit(solution)/shard_map/last/pallas_call | solution.py:680
  (54 shorter events, 0.3 us)
Async XLA Ops:
  0.6 1.2 copy-start
  1.8 9.0 %collective-permute-start = (bf16[1,96,512]{2,1,0:T(8,128)(2,1)S(1)}, bf16[1,96,512]{2,1,0:T(8,128)(2,1)S(1)}, u32[]{:S(2)}, u32[]{:S(2)}) collective-permute-start(bf16[1,96,512]{2,1,0:T(8,128)(2,1)S(1)} %fusion.4), channel_id=1, source_target_pairs={{0,2},{1,3},{2,0},{3,1},{4,6},{5,7},{6,4},{7,5},{8,10},{9,11},{10,... | collective-permute-start | bytes 294920 | tf_op jit(solution)/shard_map/ppermute | solution.py:459
  10.9 7.1 %collective-permute-start.1 = (bf16[2,96,512]{2,1,0:T(8,128)(2,1)S(1)}, bf16[2,96,512]{2,1,0:T(8,128)(2,1)S(1)}, u32[]{:S(2)}, u32[]{:S(2)}) collective-permute-start(bf16[2,96,512]{2,1,0:T(8,128)(2,1)S(1)} %pad_maximum_fusion.2), channel_id=1, source_target_pairs={{0,1},{1,0},{2,3},{3,2},{4,5},{5,4},{6,7},{7,6},{8,9},{9,8},{10,11... | collective-permute-start | bytes 589832 | tf_op jit(solution)/shard_map/ppermute | solution.py:459
  13.8 40.4 %collective-permute-start.21 = (bf16[768,256]{1,0:T(8,128)(2,1)}, bf16[768,256]{1,0:T(8,128)(2,1)}, u32[]{:S(2)}, u32[]{:S(2)}) collective-permute-start(bf16[768,256]{1,0:T(8,128)(2,1)} %get-tuple-element.46), channel_id=1, source_target_pairs={{0,1},{1,0},{2,3},{3,2},{4,5},{5,4},{6,7},{7,6},{8,9},{9,8},{10,11... | collective-permute-start | bytes 1179656 | tf_op jit(solution)/shard_map/ppermute | solution.py:459
  15.2 24.6 %collective-permute-start.10 = (bf16[1280,256]{1,0:T(8,128)(2,1)}, bf16[1280,256]{1,0:T(8,128)(2,1)S(1)}, u32[]{:S(2)}, u32[]{:S(2)}) collective-permute-start(bf16[1280,256]{1,0:T(8,128)(2,1)} %get-tuple-element.43), channel_id=1, source_target_pairs={{0,1},{1,0},{2,3},{3,2},{4,5},{5,4},{6,7},{7,6},{8,9},{9,8},{10,11... | collective-permute-start | bytes 1966088 | tf_op jit(solution)/shard_map/ppermute | solution.py:459
  19.2 26.3 %copy-start.10 = (bf16[368,512]{1,0:T(8,128)(2,1)}, bf16[368,512]{1,0:T(8,128)(2,1)S(1)}, u32[]{:S(2)}) copy-start(bf16[368,512]{1,0:T(8,128)(2,1)S(1)} %fusion.1.refs_0_) | copy-start | bytes 1130500
  19.2 27.9 %collective-permute-start.2 = (bf16[368,512]{1,0:T(8,128)(2,1)S(1)}, bf16[368,512]{1,0:T(8,128)(2,1)}, u32[]{:S(2)}, u32[]{:S(2)}) collective-permute-start(bf16[368,512]{1,0:T(8,128)(2,1)S(1)} %fusion.1.refs_0_), channel_id=1, source_target_pairs={{0,8},{4,12},{8,0},{12,4},{16,24},{20,28},{24,16},{28,20},{1,9},{5... | collective-permute-start | bytes 1130504 | tf_op jit(solution)/shard_map/ppermute | solution.py:459
  21.3 18.5 %copy-start.1 = (bf16[256,512]{1,0:T(8,128)(2,1)S(1)}, bf16[256,512]{1,0:T(8,128)(2,1)}, u32[]{:S(2)}) copy-start(bf16[256,512]{1,0:T(8,128)(2,1)} %cot_ref.7) | copy-start | bytes 786436
  21.3 18.5 %copy-start.4 = (f32[512,128]{1,0:T(8,128)S(1)}, f32[512,128]{1,0:T(8,128)}, u32[]{:S(2)}) copy-start(f32[512,128]{1,0:T(8,128)} %constant.108.clone.into_ref) | copy-start | bytes 786436
  21.3 18.5 %copy-start.6 = (bf16[768,256]{1,0:T(8,128)(2,1)S(1)}, bf16[768,256]{1,0:T(8,128)(2,1)}, u32[]{:S(2)}) copy-start(bf16[768,256]{1,0:T(8,128)(2,1)} %get-tuple-element.42.act_ref) | copy-start | bytes 1179652
  21.3 18.5 %copy-start.8 = (f32[64,32]{1,0:T(8,128)S(1)}, f32[64,32]{1,0:T(8,128)}, u32[]{:S(2)}) copy-start(f32[64,32]{1,0:T(8,128)} %constant.107.clone.split_ref) | copy-start | bytes 24580
  26.1 21.4 %copy-start.19 = (s32[64,128]{1,0:T(8,128)S(1)}, s32[64,128]{1,0:T(8,128)}, u32[]{:S(2)}) copy-start(s32[64,128]{1,0:T(8,128)} %constant.109.clone) | copy-start | bytes 98308
  26.2 21.4 %copy-start.20 = (f32[64,128]{1,0:T(8,128)S(1)}, f32[64,128]{1,0:T(8,128)}, u32[]{:S(2)}) copy-start(f32[64,128]{1,0:T(8,128)} %get-tuple-element.40) | copy-start | bytes 98308
  26.2 19.3 %collective-permute-start.9 = (f32[64,128]{1,0:T(8,128)}, f32[64,128]{1,0:T(8,128)S(1)}, u32[]{:S(2)}, u32[]{:S(2)}) collective-permute-start(f32[64,128]{1,0:T(8,128)} %get-tuple-element.41), channel_id=1, source_target_pairs={{0,1},{1,0},{2,3},{3,2},{4,5},{5,4},{6,7},{7,6},{8,9},{9,8},{10,11... | collective-permute-start | bytes 98312 | tf_op jit(solution)/shard_map/ppermute | solution.py:459
  39.8 63.3 %copy-start.3 = (bf16[1280,256]{1,0:T(8,128)(2,1)}, bf16[1280,256]{1,0:T(8,128)(2,1)S(1)}, u32[]{:S(2)}) copy-start(bf16[1280,256]{1,0:T(8,128)(2,1)S(1)} %collective-permute-done.10.sent_ref) | copy-start | bytes 1966084
  41.5 6.0 %collective-permute-start.11 = (f32[64,128]{1,0:T(8,128)S(1)}, f32[64,128]{1,0:T(8,128)S(1)}, u32[]{:S(2)}, u32[]{:S(2)}) collective-permute-start(f32[64,128]{1,0:T(8,128)S(1)} %get-tuple-element.44), channel_id=1, source_target_pairs={{0,2},{1,3},{2,0},{3,1},{4,6},{5,7},{6,4},{7,5},{8,10},{9,11},{10,... | collective-permute-start | bytes 98312 | tf_op jit(solution)/shard_map/ppermute | solution.py:459
  45.4 10.8 %collective-permute-start.5 = (bf16[368,512]{1,0:T(8,128)(2,1)S(1)}, bf16[368,512]{1,0:T(8,128)(2,1)S(1)}, u32[]{:S(2)}, u32[]{:S(2)}) collective-permute-start(bf16[368,512]{1,0:T(8,128)(2,1)S(1)} %fusion.1.refs_0_), channel_id=1, source_target_pairs={{0,4},{4,0},{8,12},{12,8},{16,20},{20,16},{24,28},{28,24},{1,5},{5... | collective-permute-start | bytes 1130504 | tf_op jit(solution)/shard_map/ppermute | solution.py:459
  45.5 11.7 %collective-permute-start.3 = (bf16[368,512]{1,0:T(8,128)(2,1)S(1)}, bf16[368,512]{1,0:T(8,128)(2,1)S(1)}, u32[]{:S(2)}, u32[]{:S(2)}) collective-permute-start(bf16[368,512]{1,0:T(8,128)(2,1)S(1)} %fusion.1.refs_0_), channel_id=1, source_target_pairs={{0,16},{4,20},{8,24},{12,28},{16,0},{20,4},{24,8},{28,12},{1,17},{... | collective-permute-start | bytes 1130504 | tf_op jit(solution)/shard_map/ppermute | solution.py:459
  47.1 34.3 %collective-permute-start.4 = (bf16[368,512]{1,0:T(8,128)(2,1)}, bf16[368,512]{1,0:T(8,128)(2,1)}, u32[]{:S(2)}, u32[]{:S(2)}) collective-permute-start(bf16[368,512]{1,0:T(8,128)(2,1)} %collective-permute-done.2.refs_1_), channel_id=1, source_target_pairs={{0,16},{4,20},{8,24},{12,28},{16,0},{20,4},{24,8},{28,12},{1,17},{... | collective-permute-start | bytes 1130504 | tf_op jit(solution)/shard_map/ppermute | solution.py:459
  47.6 55.5 %copy-start.16 = (bf16[64,128]{1,0:T(8,128)(2,1)}, bf16[64,128]{1,0:T(8,128)(2,1)S(1)}, u32[]{:S(2)}) copy-start(bf16[64,128]{1,0:T(8,128)(2,1)S(1)} %select_convert_fusion.quad_ref) | copy-start | bytes 49156
  47.6 4.9 %collective-permute-start.12 = (bf16[1,64,128]{2,1,0:T(8,128)(2,1)S(1)}, bf16[1,64,128]{2,1,0:T(8,128)(2,1)S(1)}, u32[]{:S(2)}, u32[]{:S(2)}) collective-permute-start(bf16[1,64,128]{2,1,0:T(8,128)(2,1)S(1)} %bitcast.49), channel_id=1, source_target_pairs={{0,2},{1,3},{2,0},{3,1},{4,6},{5,7},{6,4},{7,5},{8,10},{9,11},{10,... | collective-permute-start | bytes 49160 | tf_op jit(solution)/shard_map/ppermute | solution.py:459
  52.5 46.8 %collective-permute-start.24 = (bf16[1920,128]{1,0:T(8,128)(2,1)S(1)}, bf16[1920,128]{1,0:T(8,128)(2,1)S(1)}, u32[]{:S(2)}, u32[]{:S(2)}) collective-permute-start(bf16[1920,128]{1,0:T(8,128)(2,1)S(1)} %get-tuple-element.49), channel_id=1, source_target_pairs={{0,2},{1,3},{2,0},{3,1},{4,6},{5,7},{6,4},{7,5},{8,10},{9,11},{10,... | collective-permute-start | bytes 1474568 | tf_op jit(solution)/shard_map/ppermute | solution.py:459
  54.3 9.5 %collective-permute-start.13 = (bf16[2,64,128]{2,1,0:T(8,128)(2,1)S(1)}, bf16[2,64,128]{2,1,0:T(8,128)(2,1)S(1)}, u32[]{:S(2)}, u32[]{:S(2)}) collective-permute-start(bf16[2,64,128]{2,1,0:T(8,128)(2,1)S(1)} %pad_maximum_fusion.4), channel_id=1, source_target_pairs={{0,1},{1,0},{2,3},{3,2},{4,5},{5,4},{6,7},{7,6},{8,9},{9,8},{10,11... | collective-permute-start | bytes 98312 | tf_op jit(solution)/shard_map/ppermute | solution.py:459
  56.2 7.6 %copy-start.12 = (bf16[368,512]{1,0:T(8,128)(2,1)}, bf16[368,512]{1,0:T(8,128)(2,1)S(1)}, u32[]{:S(2)}) copy-start(bf16[368,512]{1,0:T(8,128)(2,1)S(1)} %collective-permute-done.5.refs_4_) | copy-start | bytes 1130500
  56.2 23.6 %collective-permute-start.22 = (bf16[384,128]{1,0:T(8,128)(2,1)S(1)}, bf16[384,128]{1,0:T(8,128)(2,1)S(1)}, u32[]{:S(2)}, u32[]{:S(2)}) collective-permute-start(bf16[384,128]{1,0:T(8,128)(2,1)S(1)} %get-tuple-element.47), channel_id=1, source_target_pairs={{0,2},{1,3},{2,0},{3,1},{4,6},{5,7},{6,4},{7,5},{8,10},{9,11},{10,... | collective-permute-start | bytes 294920 | tf_op jit(solution)/shard_map/ppermute | solution.py:459
  57.2 42.1 %copy-start.13 = (bf16[368,512]{1,0:T(8,128)(2,1)}, bf16[368,512]{1,0:T(8,128)(2,1)S(1)}, u32[]{:S(2)}) copy-start(bf16[368,512]{1,0:T(8,128)(2,1)S(1)} %collective-permute-done.3.refs_2_) | copy-start | bytes 1130500
  57.2 42.0 %collective-permute-start.6 = (bf16[368,512]{1,0:T(8,128)(2,1)}, bf16[368,512]{1,0:T(8,128)(2,1)S(1)}, u32[]{:S(2)}, u32[]{:S(2)}) collective-permute-start(bf16[368,512]{1,0:T(8,128)(2,1)} %collective-permute-done.2.refs_1_), channel_id=1, source_target_pairs={{0,4},{4,0},{8,12},{12,8},{16,20},{20,16},{24,28},{28,24},{1,5},{5... | collective-permute-start | bytes 1130504 | tf_op jit(solution)/shard_map/ppermute | solution.py:459
  63.7 34.9 %collective-permute-start.7 = (bf16[368,512]{1,0:T(8,128)(2,1)S(1)}, bf16[368,512]{1,0:T(8,128)(2,1)S(1)}, u32[]{:S(2)}, u32[]{:S(2)}) collective-permute-start(bf16[368,512]{1,0:T(8,128)(2,1)S(1)} %collective-permute-done.3.refs_2_), channel_id=1, source_target_pairs={{0,4},{4,0},{8,12},{12,8},{16,20},{20,16},{24,28},{28,24},{1,5},{5... | collective-permute-start | bytes 1130504 | tf_op jit(solution)/shard_map/ppermute | solution.py:459
  79.8 23.3 %copy-start.18 = (bf16[384,128]{1,0:T(8,128)(2,1)}, bf16[384,128]{1,0:T(8,128)(2,1)S(1)}, u32[]{:S(2)}) copy-start(bf16[384,128]{1,0:T(8,128)(2,1)S(1)} %collective-permute-done.22.rest_0_) | copy-start | bytes 294916
  79.8 4.3 %collective-permute-start.15 = (bf16[4,64,128]{2,1,0:T(8,128)(2,1)S(1)}, bf16[4,64,128]{2,1,0:T(8,128)(2,1)S(1)}, u32[]{:S(2)}, u32[]{:S(2)}) collective-permute-start(bf16[4,64,128]{2,1,0:T(8,128)(2,1)S(1)} %pad_maximum_fusion.3.refs_0_), channel_id=1, source_target_pairs={{0,16},{4,20},{8,24},{12,28},{16,0},{20,4},{24,8},{28,12},{1,17},{... | collective-permute-start | bytes 196616 | tf_op jit(solution)/shard_map/ppermute | solution.py:459
  81.3 27.0 %collective-permute-start.8 = (bf16[368,512]{1,0:T(8,128)(2,1)}, bf16[368,512]{1,0:T(8,128)(2,1)}, u32[]{:S(2)}, u32[]{:S(2)}) collective-permute-start(bf16[368,512]{1,0:T(8,128)(2,1)} %collective-permute-done.4.refs_3_), channel_id=1, source_target_pairs={{0,4},{4,0},{8,12},{12,8},{16,20},{20,16},{24,28},{28,24},{1,5},{5... | collective-permute-start | bytes 1130504 | tf_op jit(solution)/shard_map/ppermute | solution.py:459
  84.1 4.3 %collective-permute-start.14 = (bf16[4,64,128]{2,1,0:T(8,128)(2,1)S(1)}, bf16[4,64,128]{2,1,0:T(8,128)(2,1)S(1)}, u32[]{:S(2)}, u32[]{:S(2)}) collective-permute-start(bf16[4,64,128]{2,1,0:T(8,128)(2,1)S(1)} %pad_maximum_fusion.3.refs_0_), channel_id=1, source_target_pairs={{0,8},{4,12},{8,0},{12,4},{16,24},{20,28},{24,16},{28,20},{1,9},{5... | collective-permute-start | bytes 196616 | tf_op jit(solution)/shard_map/ppermute | solution.py:459
  88.3 6.1 %collective-permute-start.23 = (bf16[576,128]{1,0:T(8,128)(2,1)S(1)}, bf16[576,128]{1,0:T(8,128)(2,1)S(1)}, u32[]{:S(2)}, u32[]{:S(2)}) collective-permute-start(bf16[576,128]{1,0:T(8,128)(2,1)S(1)} %get-tuple-element.48), channel_id=1, source_target_pairs={{0,2},{1,3},{2,0},{3,1},{4,6},{5,7},{6,4},{7,5},{8,10},{9,11},{10,... | collective-permute-start | bytes 442376 | tf_op jit(solution)/shard_map/ppermute | solution.py:459
  94.4 8.7 %copy-start.17 = (bf16[576,128]{1,0:T(8,128)(2,1)}, bf16[576,128]{1,0:T(8,128)(2,1)S(1)}, u32[]{:S(2)}) copy-start(bf16[576,128]{1,0:T(8,128)(2,1)S(1)} %collective-permute-done.23.rest_1_) | copy-start | bytes 442372
  94.4 4.3 %collective-permute-start.19 = (bf16[4,64,128]{2,1,0:T(8,128)(2,1)S(1)}, bf16[4,64,128]{2,1,0:T(8,128)(2,1)S(1)}, u32[]{:S(2)}, u32[]{:S(2)}) collective-permute-start(bf16[4,64,128]{2,1,0:T(8,128)(2,1)S(1)} %collective-permute-done.14.refs_1_), channel_id=1, source_target_pairs={{0,16},{4,20},{8,24},{12,28},{16,0},{20,4},{24,8},{28,12},{1,17},{... | collective-permute-start | bytes 196616 | tf_op jit(solution)/shard_map/ppermute | solution.py:459
  98.7 13.7 %collective-permute-start.16 = (bf16[4,64,128]{2,1,0:T(8,128)(2,1)S(1)}, bf16[4,64,128]{2,1,0:T(8,128)(2,1)S(1)}, u32[]{:S(2)}, u32[]{:S(2)}) collective-permute-start(bf16[4,64,128]{2,1,0:T(8,128)(2,1)S(1)} %pad_maximum_fusion.3.refs_0_), channel_id=1, source_target_pairs={{0,4},{4,0},{8,12},{12,8},{16,20},{20,16},{24,28},{28,24},{1,5},{5... | collective-permute-start | bytes 196616 | tf_op jit(solution)/shard_map/ppermute | solution.py:459
  98.7 1.1 copy-start.15
  98.7 13.7 %collective-permute-start.17 = (bf16[4,64,128]{2,1,0:T(8,128)(2,1)S(1)}, bf16[4,64,128]{2,1,0:T(8,128)(2,1)S(1)}, u32[]{:S(2)}, u32[]{:S(2)}) collective-permute-start(bf16[4,64,128]{2,1,0:T(8,128)(2,1)S(1)} %collective-permute-done.14.refs_1_), channel_id=1, source_target_pairs={{0,4},{4,0},{8,12},{12,8},{16,20},{20,16},{24,28},{28,24},{1,5},{5... | collective-permute-start | bytes 196616 | tf_op jit(solution)/shard_map/ppermute | solution.py:459
  99.2 9.1 %copy-start.14 = (bf16[368,512]{1,0:T(8,128)(2,1)}, bf16[368,512]{1,0:T(8,128)(2,1)S(1)}, u32[]{:S(2)}) copy-start(bf16[368,512]{1,0:T(8,128)(2,1)S(1)} %collective-permute-done.6.refs_5_) | copy-start | bytes 1130500
  99.2 13.2 %collective-permute-start.18 = (bf16[4,64,128]{2,1,0:T(8,128)(2,1)S(1)}, bf16[4,64,128]{2,1,0:T(8,128)(2,1)S(1)}, u32[]{:S(2)}, u32[]{:S(2)}) collective-permute-start(bf16[4,64,128]{2,1,0:T(8,128)(2,1)S(1)} %collective-permute-done.15.refs_2_), channel_id=1, source_target_pairs={{0,4},{4,0},{8,12},{12,8},{16,20},{20,16},{24,28},{28,24},{1,5},{5... | collective-permute-start | bytes 196616 | tf_op jit(solution)/shard_map/ppermute | solution.py:459
  99.3 3.9 %copy-start.11 = (bf16[1920,128]{1,0:T(8,128)(2,1)}, bf16[1920,128]{1,0:T(8,128)(2,1)S(1)}, u32[]{:S(2)}) copy-start(bf16[1920,128]{1,0:T(8,128)(2,1)S(1)} %collective-permute-done.24.rest_2_) | copy-start | bytes 1474564
  99.3 13.1 %collective-permute-start.20 = (bf16[4,64,128]{2,1,0:T(8,128)(2,1)S(1)}, bf16[4,64,128]{2,1,0:T(8,128)(2,1)S(1)}, u32[]{:S(2)}, u32[]{:S(2)}) collective-permute-start(bf16[4,64,128]{2,1,0:T(8,128)(2,1)S(1)} %collective-permute-done.19.refs_6_), channel_id=1, source_target_pairs={{0,4},{4,0},{8,12},{12,8},{16,20},{20,16},{24,28},{28,24},{1,5},{5... | collective-permute-start | bytes 196616 | tf_op jit(solution)/shard_map/ppermute | solution.py:459
  108.3 4.1 %copy-start.2 = (bf16[256,1536]{1,0:T(8,128)(2,1)S(1)}, bf16[256,1536]{1,0:T(8,128)(2,1)}, u32[]{:S(2)}) copy-start(bf16[256,1536]{1,0:T(8,128)(2,1)} %lows.1.lows_ref) | copy-start | bytes 2359300
  108.3 4.1 %copy-start.7 = (bf16[256,512]{1,0:T(8,128)(2,1)S(1)}, bf16[256,512]{1,0:T(8,128)(2,1)}, u32[]{:S(2)}) copy-start(bf16[256,512]{1,0:T(8,128)(2,1)} %constant.112.clone.across_ref) | copy-start | bytes 786436
  112.4 1.0 copy-start.5
  113.4 0.7 copy-start.9

commit v2 on v1

--- a/solution.py
+++ b/solution.py
@@ -279,17 +279,26 @@
             tiled_ref[place, :] = tiled_ref[place, :] - rebuilt[:, g * LANES : (g + 1) * LANES]
     copy.wait()
     first = 0
-    for ref in sums:
-        for c in range(0, ref.shape[0], 2 * KEEP):
-            n = min(2 * KEEP, ref.shape[0] - c)
+    for ref in sums + (None,):
+        size = out_ref.shape[0] - first if ref is None else ref.shape[0]
+        for c in range(0, size, 2 * KEEP):
+            n = min(2 * KEEP, size - c)
             rows = slice(first + c, first + c + n)
             at = pl.ds(pl.multiple_of(skip * KEEP + first + c, KEEP), n)
-            out_ref[rows, :] = (
-                momentum_decay * held_ref[rows, :]
-                + tiled_ref[at, :]
-                + ref[c : c + n, :].astype(jnp.float32)
-            )
-        first += ref.shape[0]
+            value = momentum_decay * held_ref[rows, :] + tiled_ref[at, :]
+            if ref is not None:
+                value = value + ref[c : c + n, :].astype(jnp.float32)
+            out_ref[rows, :] = value
+        first += size
+
+
+def finish_kernel(base_ref, sum_ref, out_ref):
+    first = base_ref.shape[0] - sum_ref.shape[0]
+    for c in range(0, base_ref.shape[0], KEEP):
+        value = base_ref[c : c + KEEP, :]
+        if c >= first:
+            value = value + sum_ref[c - first : c - first + KEEP, :].astype(jnp.float32)
+        out_ref[c : c + KEEP, :] = value
 
 
 def first_row(shard, tiles_here, col_tiles):
@@ -328,23 +337,17 @@
 def unchanged_kernel(inputs_ref, *refs, tiles_here, list_row):
     count = len(HELD_ORDER)
     held, (out_ref, place_ref), rest = refs[:count], refs[count : count + 2], refs[count + 2 :]
-    mine_ref, held_refs, sems = rest[0], rest[1:-1], rest[-1]
+    (mine_ref, sems), held_refs = rest, held
     rep, me = lax.axis_index("replica"), lax.axis_index("tok")
     used = inputs_ref.shape[0]
     mine_copies = [
         pltpu.make_async_copy(
-            inputs_ref.at[:, rep ^ o], mine_ref.at[n, pl.ds(0, used)], sems.at[count + n]
+            inputs_ref.at[:, rep ^ o], mine_ref.at[n, pl.ds(0, used)], sems.at[n]
         )
         for n, o in enumerate(SHARE_ORDER)
     ]
-    copies = [
-        pltpu.make_async_copy(a, b, sems.at[n]) for n, (a, b) in enumerate(zip(held, held_refs))
-    ]
-    for n, o in enumerate(SHARE_ORDER):
-        mine_copies[n].start()
-        for copy, k in zip(copies, HELD_ORDER):
-            if k == o:
-                copy.start()
+    for copy in mine_copies:
+        copy.start()
     for n in range(used, mine_ref.shape[1]):
         mine_ref[:, n] = jnp.zeros_like(mine_ref[:, n])
     size = held_refs[0].shape[0]
@@ -354,10 +357,9 @@
         mine_copies[n].wait()
         x = mine_ref[n].reshape(size, mine_ref.shape[3])
         first = 0
-        for copy, k, piece in zip(copies, HELD_ORDER, held_refs):
+        for k, piece in zip(HELD_ORDER, held_refs):
             if k != o:
                 continue
-            copy.wait()
             term = lax.dot_general(
                 x[first : first + piece.shape[0], :], piece[...], (((0,), (0,)), ((), ())),
                 preferred_element_type=jnp.float32,
@@ -414,14 +416,22 @@
             pltpu.store(place, value, mask=mask)
         return carry
 
-    lax.fori_loop(0, quads_ref.shape[0], add_list, 0)
-
-
-def last_kernel(place_ref, lows_ref, base_ref, across_ref, *refs):
-    quads, (out_ref, sum_ref) = refs[:-2], refs[-2:]
+    lax.fori_loop(0, quads_ref.shape[0], add_list, 0, unroll=4)
+
+
+def last_kernel(place_ref, lows_in, base_in, across_ref, *refs):
+    quads, (out_ref, sum_ref, lows_ref, base_ref, sems) = refs[:-5], refs[-5:]
+    copies = [
+        pltpu.make_async_copy(lows_in, lows_ref, sems.at[0]),
+        pltpu.make_async_copy(base_in, base_ref, sems.at[1]),
+    ]
+    for copy in copies:
+        copy.start()
     sum_ref[...] = jnp.zeros_like(sum_ref)
     for n, ref in enumerate(quads):
         add_quads(place_ref, n, ref, sum_ref)
+    for copy in copies:
+        copy.wait()
     rows = lows_ref.shape[1]
     whole = jnp.concatenate(
         [
@@ -608,18 +618,27 @@
     quads = jnp.where(
         jnp.asarray(at, jnp.int32) < counts[0, 0], low_mine + low_from_near + low_from_far, 0.0
     ).astype(jnp.bfloat16)
-    new_momentum = pl.pallas_call(
+    begun = pl.pallas_call(
         functools.partial(own_kernel, scale=scale, spans=spans, tiles_here=tiles_here),
         out_shape=jax.ShapeDtypeStruct(moment.shape, jnp.float32),
-        in_specs=smem(1) + [anywhere] + vmem(7 + len(cuts)),
+        in_specs=smem(1) + [anywhere] + vmem(6 + len(cuts)),
         out_specs=vmem(1)[0],
         scratch_shapes=grid_scratch
         + [pltpu.VMEM(moment.shape, jnp.float32), pltpu.SemaphoreType.DMA((1,))],
+        compiler_params=room(16),
         name="own",
     )(
         chosen[0, 0], moment, mine_near, cotangent, sent_far, sent_near, quads, split_back,
-        back, *sums_from,
-    ).reshape(momentum.shape)
+        back, *sums_from[:-1],
+    )
+    new_momentum = pl.pallas_call(
+        finish_kernel,
+        out_shape=jax.ShapeDtypeStruct(moment.shape, jnp.float32),
+        in_specs=vmem(2),
+        out_specs=vmem(1)[0],
+        compiler_params=room(12),
+        name="finish",
+    )(begun, sums_from[-1]).reshape(momentum.shape)
 
     whole = jnp.concatenate(
         [
@@ -650,13 +669,13 @@
             jax.ShapeDtypeStruct((tokens, width), jnp.float32),
             jax.ShapeDtypeStruct((replicas, LANES), jnp.int32),
         ],
-        in_specs=[anywhere] * (1 + len(held_all)),
+        in_specs=[anywhere] + vmem(len(held_all)),
         out_specs=vmem(2),
         scratch_shapes=[
             pltpu.VMEM((replicas, held[0].shape[0] // rows_share, rows_share, tokens), jnp.bfloat16)
         ]
-        + [pltpu.VMEM(h.shape, jnp.bfloat16) for h in held_all]
-        + [pltpu.SemaphoreType.DMA((replicas + len(held_all),))],
+        + [pltpu.SemaphoreType.DMA((replicas,))],
+        compiler_params=room(12),
         name="unchanged",
     )(by_share, *held_all)
 
@@ -680,9 +699,14 @@
     values = pl.pallas_call(
         last_kernel,
         out_shape=jax.ShapeDtypeStruct((tokens, width), jnp.bfloat16),
-        in_specs=smem(1) + vmem(3 + len(SHARE_ORDER)),
+        in_specs=smem(1) + [anywhere] * 2 + vmem(1 + len(SHARE_ORDER)),
         out_specs=vmem(1)[0],
-        scratch_shapes=[pltpu.VMEM((col_tiles // 4 * sum_rows, LANES), jnp.float32)],
+        scratch_shapes=[
+            pltpu.VMEM((col_tiles // 4 * sum_rows, LANES), jnp.float32),
+            pltpu.VMEM(lows.shape, lows.dtype),
+            pltpu.VMEM(unchanged.shape, unchanged.dtype),
+            pltpu.SemaphoreType.DMA((2,)),
+        ],
         compiler_params=room(12),
         name="last",
     )(places, lows, unchanged, across.astype(jnp.bfloat16), *[brought[o] for o in SHARE_ORDER])

time: 119 us -> 126 us (1.059)
  local copies, waits for them, and re-layouts: 3.21 us -> 14.1 us
  Pallas kernels: 28 us -> 24.4 us
  waiting for transfers between devices: 57 us -> 54.4 us
  other arithmetic: 1.53 us -> 2.82 us
    unnamed x43 -> x65, local copies, waits for them, and re-layouts: 2.21 us -> 13.1 us
    pallas_call x1, Pallas kernels: 5.11 us -> 2.49 us  [four_shards(): pl.pallas_call(functools.partial(own_kernel, scale=scale, spans=spans, ti...]
    ppermute x25, waiting for transfers between devices: 57 us -> 54.4 us  [swap(): return lax.ppermute(array, axis, [(i, i ^ bit) for i in range(size)])]
    pallas_call x1, Pallas kernels: 4.87 us -> 3.19 us  [four_shards(): pl.pallas_call(last_kernel, out_shape=jax.ShapeDtypeStruct((tokens, width...]
  transfers between devices with their start and end apart: 25 -> 25, of which waited for: 10 -> 9; matrix products, arithmetic and copies ran while one was open for 1% -> 2% of each run, Pallas kernels for 19% -> 17%
where the time goes in v2:
time: 126 us; the launch traced here: 125 us
  waiting for transfers between devices  54.4 us (43%)
  starting transfers between devices  27.7 us (22%)
  Pallas kernels  24.4 us (19%)
  local copies, waits for them, and re-layouts  14.1 us (11%)
  other arithmetic  2.82 us (2%)
  between operations  1.67 us (1%)
    ppermute x25, waiting for transfers between devices, swap(): return lax.ppermute(array, axis, [(i, i ^ bit) for i in range(size)])  54.4 us
    ppermute x25, starting transfers between devices, swap(): return lax.ppermute(array, axis, [(i, i ^ bit) for i in range(size)])  27.7 us
    unnamed x65, local copies, waits for them, and re-layouts  13.1 us
    pallas_call x1, Pallas kernels, four_shards(): pl.pallas_call(functools.partial(factor_lows_kernel, scale=scale, tiles_h...  4.79 us
    pallas_call x1, Pallas kernels, four_shards(): pl.pallas_call(functools.partial(unchanged_kernel, tiles_here=tiles_here,...  3.41 us
    pallas_call x1, Pallas kernels, four_shards(): pl.pallas_call(functools.partial(lows_kernel, span=at_once * TILE), out_s...  3.39 us
    pallas_call x1, Pallas kernels, four_shards(): pl.pallas_call(last_kernel, out_shape=jax.ShapeDtypeStruct((tokens, width...  3.19 us
  transfers between devices with their start and end apart: 25, of which 9 were waited for; matrix products, arithmetic and copies ran while one was open for 2% of the time, Pallas kernels for 17%

profile of v2, /device:TPU:0, one launch (start us, length us, event | category | flops | bytes accessed | tf_op | source)
XLA Modules:
  0.0 125.0 jit_solution(373398361665304963)
XLA Ops:
  0.7 0.7 convert_bitcast_fusion
  1.4 0.4 copy-done
  1.8 4.1 %collective-permute-start = (bf16[1,96,512]{2,1,0:T(8,128)(2,1)S(1)}, bf16[1,96,512]{2,1,0:T(8,128)(2,1)S(1)}, u32[]{:S(2)}, u32[]{:S(2)}) collective-permute-start(bf16[1,96,512]{2,1,0:T(8,128)(2,1)S(1)} %fusion.4), channel_id=1, source_target_pairs={{0,2},{1,3},{2,0},{3,1},{4,6},{5,7},{6,4},{7,5},{8,10},{9,11},{10,... | collective-permute-start | bytes 294920 | tf_op jit(solution)/shard_map/ppermute | solution.py:469
  5.9 4.9 %collective-permute-done = bf16[1,96,512]{2,1,0:T(8,128)(2,1)S(1)} collective-permute-done((bf16[1,96,512]{2,1,0:T(8,128)(2,1)S(1)}, bf16[1,96,512]{2,1,0:T(8,128)(2,1)S(1)}, u32[]{:S(2)}, u32[]{:S(2)}) %collective-permute-start) | collective-permute-done | bytes 98336 | tf_op jit(solution)/shard_map/ppermute | solution.py:469
  10.9 0.8 collective-permute-start.1
  11.6 2.2 %prepare.1 = (bf16[1280,256]{1,0:T(8,128)(2,1)}, bf16[768,256]{1,0:T(8,128)(2,1)}) custom-call(bf16[2880,256]{1,0:T(8,128)(2,1)} %bitcast.49, bf16[256,512]{1,0:T(8,128)(2,1)} %cot_ref.7), custom_call_target="tpu_custom_call" | custom-call | tf_op jit(solution)/shard_map/prepare/pallas_call | solution.py:546
  13.8 1.4 %collective-permute-start.21 = (bf16[768,256]{1,0:T(8,128)(2,1)}, bf16[768,256]{1,0:T(8,128)(2,1)}, u32[]{:S(2)}, u32[]{:S(2)}) collective-permute-start(bf16[768,256]{1,0:T(8,128)(2,1)} %get-tuple-element.46), channel_id=1, source_target_pairs={{0,1},{1,0},{2,3},{3,2},{4,5},{5,4},{6,7},{7,6},{8,9},{9,8},{10,11... | collective-permute-start | bytes 1179656 | tf_op jit(solution)/shard_map/ppermute | solution.py:469
  15.2 0.7 collective-permute-start.10
  15.9 2.0 %mine.1 = (bf16[768,256]{1,0:T(8,128)(2,1)}, bf16[768,256]{1,0:T(8,128)(2,1)}) custom-call(bf16[2880,256]{1,0:T(8,128)(2,1)} %bitcast.50), custom_call_target="tpu_custom_call" | custom-call | tf_op jit(solution)/shard_map/mine/pallas_call | solution.py:558
  18.1 0.6 copy-done.29
  18.7 0.1 pad_maximum_fusion.1
  18.8 0.4 reshape.93
  19.2 0.1 copy.26
  19.3 0.4 reshape.94
  19.8 1.6 %collective-permute-start.2 = (bf16[368,512]{1,0:T(8,128)(2,1)S(1)}, bf16[368,512]{1,0:T(8,128)(2,1)}, u32[]{:S(2)}, u32[]{:S(2)}) collective-permute-start(bf16[368,512]{1,0:T(8,128)(2,1)S(1)} %fusion.1.refs_0_), channel_id=1, source_target_pairs={{0,8},{4,12},{8,0},{12,4},{16,24},{20,28},{24,16},{28,20},{1,9},{5... | collective-permute-start | bytes 1130504 | tf_op jit(solution)/shard_map/ppermute | solution.py:469
  21.4 1.3 %fusion.6.other_ref = s32[8]{0:T(128)} fusion(bf16[2,96,512]{2,1,0:T(8,128)(2,1)} %copy-done.29), kind=kLoop, calls=%fused_computation.23 | loop fusion | flops 8 | bytes 48 | tf_op jit(solution)/shard_map/convert_element_type | solution.py:567
  22.6 4.8 %factor_lows.1 = (f32[64,128]{1,0:T(8,128)}, f32[64,128]{1,0:T(8,128)}) custom-call(s32[8]{0:T(128)} %bitcast.47, s32[8]{0:T(128)} %fusion.6.other_ref, f32[2880,128]{1,0:T(8,128)} %bitcast.42, bf16[2880,256]{1,0:T(8,128)(2,1)} %bitcast.51, bf16[256,512]{1,0:T(8,128)(2,1)} %cot_ref.7, bf16[160,320]{1,0:T(8,128)(2,1)} %constant.103.clone.high_ref.along_high_ref, ...), custom_call_target="tpu_custom_call" | custom-call | tf_op jit(solution)/shard_map/factor_lows/pallas_call | solution.py:578
  27.5 1.5 %collective-permute-start.9 = (f32[64,128]{1,0:T(8,128)}, f32[64,128]{1,0:T(8,128)S(1)}, u32[]{:S(2)}, u32[]{:S(2)}) collective-permute-start(f32[64,128]{1,0:T(8,128)} %get-tuple-element.41), channel_id=1, source_target_pairs={{0,1},{1,0},{2,3},{3,2},{4,5},{5,4},{6,7},{7,6},{8,9},{9,8},{10,11... | collective-permute-start | bytes 98312 | tf_op jit(solution)/shard_map/ppermute | solution.py:469
  28.9 10.9 %collective-permute-done.10.sent_ref = bf16[1280,256]{1,0:T(8,128)(2,1)S(1)} collective-permute-done((bf16[1280,256]{1,0:T(8,128)(2,1)}, bf16[1280,256]{1,0:T(8,128)(2,1)S(1)}, u32[]{:S(2)}, u32[]{:S(2)}) %collective-permute-start.10) | collective-permute-done | bytes 655392 | tf_op jit(solution)/shard_map/ppermute | solution.py:469
  39.8 1.7 %far.1 = (f32[64,128]{1,0:T(8,128)S(1)}, bf16[384,128]{1,0:T(8,128)(2,1)S(1)}, bf16[576,128]{1,0:T(8,128)(2,1)S(1)}, bf16[1920,128]{1,0:T(8,128)(2,1)S(1)}) custom-call(s32[8]{0:T(128)S(1)} %fusion.5.chosen_ref, bf16[768,256]{1,0:T(8,128)(2,1)S(1)} %copy-done.8, bf16[256,512]{1,0:T(8,128)(2,1)S(1)} %copy-done.3, ...), custom_call_target="tpu_custom_call" | custom-call | tf_op jit(solution)/shard_map/far/pallas_call | solution.py:602
  41.5 3.2 %collective-permute-start.11 = (f32[64,128]{1,0:T(8,128)S(1)}, f32[64,128]{1,0:T(8,128)S(1)}, u32[]{:S(2)}, u32[]{:S(2)}) collective-permute-start(f32[64,128]{1,0:T(8,128)S(1)} %get-tuple-element.44), channel_id=1, source_target_pairs={{0,2},{1,3},{2,0},{3,1},{4,6},{5,7},{6,4},{7,5},{8,10},{9,11},{10,... | collective-permute-start | bytes 98312 | tf_op jit(solution)/shard_map/ppermute | solution.py:469
  45.4 0.1 collective-permute-start.5
  45.5 1.6 %collective-permute-start.3 = (bf16[368,512]{1,0:T(8,128)(2,1)S(1)}, bf16[368,512]{1,0:T(8,128)(2,1)S(1)}, u32[]{:S(2)}, u32[]{:S(2)}) collective-permute-start(bf16[368,512]{1,0:T(8,128)(2,1)S(1)} %fusion.1.refs_0_), channel_id=1, source_target_pairs={{0,16},{4,20},{8,24},{12,28},{16,0},{20,4},{24,8},{28,12},{1,17},{... | collective-permute-start | bytes 1130504 | tf_op jit(solution)/shard_map/ppermute | solution.py:469
  47.1 0.5 collective-permute-start.4
  47.6 2.0 %collective-permute-start.12 = (bf16[1,64,128]{2,1,0:T(8,128)(2,1)S(1)}, bf16[1,64,128]{2,1,0:T(8,128)(2,1)S(1)}, u32[]{:S(2)}, u32[]{:S(2)}) collective-permute-start(bf16[1,64,128]{2,1,0:T(8,128)(2,1)S(1)} %bitcast.44), channel_id=1, source_target_pairs={{0,2},{1,3},{2,0},{3,1},{4,6},{5,7},{6,4},{7,5},{8,10},{9,11},{10,... | collective-permute-start | bytes 49160 | tf_op jit(solution)/shard_map/ppermute | solution.py:469
  49.6 2.7 %collective-permute-done.12 = bf16[1,64,128]{2,1,0:T(8,128)(2,1)S(1)} collective-permute-done((bf16[1,64,128]{2,1,0:T(8,128)(2,1)S(1)}, bf16[1,64,128]{2,1,0:T(8,128)(2,1)S(1)}, u32[]{:S(2)}, u32[]{:S(2)}) %collective-permute-start.12) | collective-permute-done | bytes 16416 | tf_op jit(solution)/shard_map/ppermute | solution.py:469
  52.3 2.0 %collective-permute-start.24 = (bf16[1920,128]{1,0:T(8,128)(2,1)S(1)}, bf16[1920,128]{1,0:T(8,128)(2,1)S(1)}, u32[]{:S(2)}, u32[]{:S(2)}) collective-permute-start(bf16[1920,128]{1,0:T(8,128)(2,1)S(1)} %get-tuple-element.49), channel_id=1, source_target_pairs={{0,2},{1,3},{2,0},{3,1},{4,6},{5,7},{6,4},{7,5},{8,10},{9,11},{10,... | collective-permute-start | bytes 1474568 | tf_op jit(solution)/shard_map/ppermute | solution.py:469
  54.3 1.9 %collective-permute-start.13 = (bf16[2,64,128]{2,1,0:T(8,128)(2,1)S(1)}, bf16[2,64,128]{2,1,0:T(8,128)(2,1)S(1)}, u32[]{:S(2)}, u32[]{:S(2)}) collective-permute-start(bf16[2,64,128]{2,1,0:T(8,128)(2,1)S(1)} %pad_maximum_fusion.4), channel_id=1, source_target_pairs={{0,1},{1,0},{2,3},{3,2},{4,5},{5,4},{6,7},{7,6},{8,9},{9,8},{10,11... | collective-permute-start | bytes 98312 | tf_op jit(solution)/shard_map/ppermute | solution.py:469
  56.2 0.7 copy-done.10
  56.9 0.9 collective-permute-start.22
  57.8 6.0 %collective-permute-done.13 = bf16[2,64,128]{2,1,0:T(8,128)(2,1)S(1)} collective-permute-done((bf16[2,64,128]{2,1,0:T(8,128)(2,1)S(1)}, bf16[2,64,128]{2,1,0:T(8,128)(2,1)S(1)}, u32[]{:S(2)}, u32[]{:S(2)}) %collective-permute-start.13) | collective-permute-done | bytes 32800 | tf_op jit(solution)/shard_map/ppermute | solution.py:469
  63.8 0.7 copy-done.12
  64.5 0.6 pad_maximum_fusion.3.refs_0_
  65.1 14.7 %collective-permute-done.22.rest_0_ = bf16[384,128]{1,0:T(8,128)(2,1)S(1)} collective-permute-done((bf16[384,128]{1,0:T(8,128)(2,1)S(1)}, bf16[384,128]{1,0:T(8,128)(2,1)S(1)}, u32[]{:S(2)}, u32[]{:S(2)}) %collective-permute-start.22) | collective-permute-done | bytes 98336 | tf_op jit(solution)/shard_map/ppermute | solution.py:469
  79.8 0.6 copy-done.25
  80.4 1.5 %collective-permute-start.15 = (bf16[4,64,128]{2,1,0:T(8,128)(2,1)}, bf16[4,64,128]{2,1,0:T(8,128)(2,1)}, u32[]{:S(2)}, u32[]{:S(2)}) collective-permute-start(bf16[4,64,128]{2,1,0:T(8,128)(2,1)} %pad_maximum_fusion.3.refs_0_), channel_id=1, source_target_pairs={{0,16},{4,20},{8,24},{12,28},{16,0},{20,4},{24,8},{28,12},{1,17},{... | collective-permute-start | bytes 196616 | tf_op jit(solution)/shard_map/ppermute | solution.py:469
  82.0 3.1 %collective-permute-done.15.refs_2_ = bf16[4,64,128]{2,1,0:T(8,128)(2,1)} collective-permute-done((bf16[4,64,128]{2,1,0:T(8,128)(2,1)}, bf16[4,64,128]{2,1,0:T(8,128)(2,1)}, u32[]{:S(2)}, u32[]{:S(2)}) %collective-permute-start.15) | collective-permute-done | bytes 65568 | tf_op jit(solution)/shard_map/ppermute | solution.py:469
  85.0 1.5 %collective-permute-start.14 = (bf16[4,64,128]{2,1,0:T(8,128)(2,1)}, bf16[4,64,128]{2,1,0:T(8,128)(2,1)}, u32[]{:S(2)}, u32[]{:S(2)}) collective-permute-start(bf16[4,64,128]{2,1,0:T(8,128)(2,1)} %pad_maximum_fusion.3.refs_0_), channel_id=1, source_target_pairs={{0,8},{4,12},{8,0},{12,4},{16,24},{20,28},{24,16},{28,20},{1,9},{5... | collective-permute-start | bytes 196616 | tf_op jit(solution)/shard_map/ppermute | solution.py:469
  86.5 3.1 %collective-permute-done.14.refs_1_ = bf16[4,64,128]{2,1,0:T(8,128)(2,1)} collective-permute-done((bf16[4,64,128]{2,1,0:T(8,128)(2,1)}, bf16[4,64,128]{2,1,0:T(8,128)(2,1)}, u32[]{:S(2)}, u32[]{:S(2)}) %collective-permute-start.14) | collective-permute-done | bytes 65568 | tf_op jit(solution)/shard_map/ppermute | solution.py:469
  89.6 6.1 %collective-permute-done.23.rest_1_ = bf16[576,128]{1,0:T(8,128)(2,1)S(1)} collective-permute-done((bf16[576,128]{1,0:T(8,128)(2,1)S(1)}, bf16[576,128]{1,0:T(8,128)(2,1)S(1)}, u32[]{:S(2)}, u32[]{:S(2)}) %collective-permute-start.23) | collective-permute-done | bytes 147488 | tf_op jit(solution)/shard_map/ppermute | solution.py:469
  95.7 0.7 copy-done.22
  96.3 1.5 %collective-permute-start.19 = (bf16[4,64,128]{2,1,0:T(8,128)(2,1)}, bf16[4,64,128]{2,1,0:T(8,128)(2,1)}, u32[]{:S(2)}, u32[]{:S(2)}) collective-permute-start(bf16[4,64,128]{2,1,0:T(8,128)(2,1)} %collective-permute-done.14.refs_1_), channel_id=1, source_target_pairs={{0,16},{4,20},{8,24},{12,28},{16,0},{20,4},{24,8},{28,12},{1,17},{... | collective-permute-start | bytes 196616 | tf_op jit(solution)/shard_map/ppermute | solution.py:469
  97.9 3.1 %collective-permute-done.19.refs_6_ = bf16[4,64,128]{2,1,0:T(8,128)(2,1)} collective-permute-done((bf16[4,64,128]{2,1,0:T(8,128)(2,1)}, bf16[4,64,128]{2,1,0:T(8,128)(2,1)}, u32[]{:S(2)}, u32[]{:S(2)}) %collective-permute-start.19) | collective-permute-done | bytes 65568 | tf_op jit(solution)/shard_map/ppermute | solution.py:469
  100.9 0.8 copy-done.16
  101.7 0.5 collective-permute-start.17
  102.2 0.8 copy-done.14
  103.0 0.8 copy-done.6
  103.8 0.5 collective-permute-start.20
  104.3 3.4 %lows.1.lows_in = bf16[256,1536]{1,0:T(8,128)(2,1)} custom-call(bf16[2880,256]{1,0:T(8,128)(2,1)} %bitcast.40, bf16[160,320]{1,0:T(8,128)(2,1)} %constant.103.clone.high_ref.along_high_ref, bf16[160,320]{1,0:T(8,128)(2,1)} %constant.104.clone.low_ref.along_low_ref), custom_call_target="tpu_custom_call" | custom-call | tf_op jit(solution)/shard_map/lows/pallas_call | solution.py:682
  107.7 1.0 copy-done.9
  108.7 0.7 copy-done.19
  109.4 0.9 copy-done.21
  110.3 0.9 copy-done.23
  111.2 0.9 copy-done.26
  112.1 0.8 copy-done.27
  112.9 0.7 copy-done.28
  113.5 2.5 %own.1.base_ref = f32[2880,128]{1,0:T(8,128)S(1)} custom-call(s32[8]{0:T(128)S(1)} %bitcast.48, f32[2880,128]{1,0:T(8,128)S(1)} %bitcast.43, bf16[768,256]{1,0:T(8,128)(2,1)S(1)} %copy-done.9, bf16[256,512]{1,0:T(8,128)(2,1)S(1)} %copy-done.3, bf16[1280,256]{1,0:T(8,128)(2,1)S(1)} %collective-permute-done.10.sent_ref, ...), custom_call_target="tpu_custom_call" | custom-call | tf_op jit(solution)/shard_map/own/pallas_call | solution.py:621
  116.1 1.2 finish.1
  117.3 0.6 copy-done.1
  118.0 0.1 copy-done.13
  118.1 0.1 copy-done.15
  118.2 0.1 copy-done.17
  118.4 3.4 %unchanged.1 = (f32[256,512]{1,0:T(8,128)S(1)}, s32[8,128]{1,0:T(8,128)S(1)}) custom-call(bf16[45,8,8,256]{3,2,1,0:T(8,128)(2,1)S(1)} %bitcast.41, bf16[368,512]{1,0:T(8,128)(2,1)S(1)} %fusion.1.refs_0_, bf16[368,512]{1,0:T(8,128)(2,1)} %collective-permute-done.2.refs_1_, bf16[368,512]{1,0:T(8,128)(2,1)S(1)} %copy-done.13, ...), custom_call_target="tpu_custom_call" | custom-call | tf_op jit(solution)/shard_map/unchanged/pallas_call | solution.py:664
  121.8 3.2 %last.1 = bf16[256,512]{1,0:T(8,128)(2,1)} custom-call(s32[8,128]{1,0:T(8,128)S(1)} %get-tuple-element.38.place_ref, bf16[256,1536]{1,0:T(8,128)(2,1)S(1)} %copy-done.4, f32[256,512]{1,0:T(8,128)S(1)} %get-tuple-element.39.base_in, bf16[256,512]{1,0:T(8,128)(2,1)S(1)} %copy-done.20, bf16[4,64,128]{2,1,0:T(8,128)(2,1)} %pad_maximum_fusion.3.refs_0_, ...), custom_call_target="tpu_custom_call" | custom-call | tf_op jit(solution)/shard_map/last/pallas_call | solution.py:699
  (77 shorter events, 0.4 us)
Async XLA Ops:
  0.6 1.2 copy-start
  1.8 9.0 %collective-permute-start = (bf16[1,96,512]{2,1,0:T(8,128)(2,1)S(1)}, bf16[1,96,512]{2,1,0:T(8,128)(2,1)S(1)}, u32[]{:S(2)}, u32[]{:S(2)}) collective-permute-start(bf16[1,96,512]{2,1,0:T(8,128)(2,1)S(1)} %fusion.4), channel_id=1, source_target_pairs={{0,2},{1,3},{2,0},{3,1},{4,6},{5,7},{6,4},{7,5},{8,10},{9,11},{10,... | collective-permute-start | bytes 294920 | tf_op jit(solution)/shard_map/ppermute | solution.py:469
  10.9 7.1 %collective-permute-start.1 = (bf16[2,96,512]{2,1,0:T(8,128)(2,1)S(1)}, bf16[2,96,512]{2,1,0:T(8,128)(2,1)S(1)}, u32[]{:S(2)}, u32[]{:S(2)}) collective-permute-start(bf16[2,96,512]{2,1,0:T(8,128)(2,1)S(1)} %pad_maximum_fusion.2), channel_id=1, source_target_pairs={{0,1},{1,0},{2,3},{3,2},{4,5},{5,4},{6,7},{7,6},{8,9},{9,8},{10,11... | collective-permute-start | bytes 589832 | tf_op jit(solution)/shard_map/ppermute | solution.py:469
  13.8 40.4 %collective-permute-start.21 = (bf16[768,256]{1,0:T(8,128)(2,1)}, bf16[768,256]{1,0:T(8,128)(2,1)}, u32[]{:S(2)}, u32[]{:S(2)}) collective-permute-start(bf16[768,256]{1,0:T(8,128)(2,1)} %get-tuple-element.46), channel_id=1, source_target_pairs={{0,1},{1,0},{2,3},{3,2},{4,5},{5,4},{6,7},{7,6},{8,9},{9,8},{10,11... | collective-permute-start | bytes 1179656 | tf_op jit(solution)/shard_map/ppermute | solution.py:469
  15.2 24.6 %collective-permute-start.10 = (bf16[1280,256]{1,0:T(8,128)(2,1)}, bf16[1280,256]{1,0:T(8,128)(2,1)S(1)}, u32[]{:S(2)}, u32[]{:S(2)}) collective-permute-start(bf16[1280,256]{1,0:T(8,128)(2,1)} %get-tuple-element.43), channel_id=1, source_target_pairs={{0,1},{1,0},{2,3},{3,2},{4,5},{5,4},{6,7},{7,6},{8,9},{9,8},{10,11... | collective-permute-start | bytes 1966088 | tf_op jit(solution)/shard_map/ppermute | solution.py:469
  18.0 0.7 copy-start.29
  19.8 27.2 %collective-permute-start.2 = (bf16[368,512]{1,0:T(8,128)(2,1)S(1)}, bf16[368,512]{1,0:T(8,128)(2,1)}, u32[]{:S(2)}, u32[]{:S(2)}) collective-permute-start(bf16[368,512]{1,0:T(8,128)(2,1)S(1)} %fusion.1.refs_0_), channel_id=1, source_target_pairs={{0,8},{4,12},{8,0},{12,4},{16,24},{20,28},{24,16},{28,20},{1,9},{5... | collective-permute-start | bytes 1130504 | tf_op jit(solution)/shard_map/ppermute | solution.py:469
  22.6 17.2 %copy-start.3 = (bf16[256,512]{1,0:T(8,128)(2,1)S(1)}, bf16[256,512]{1,0:T(8,128)(2,1)}, u32[]{:S(2)}) copy-start(bf16[256,512]{1,0:T(8,128)(2,1)} %cot_ref.7) | copy-start | bytes 786436
  22.6 17.2 %copy-start.5 = (f32[512,128]{1,0:T(8,128)S(1)}, f32[512,128]{1,0:T(8,128)}, u32[]{:S(2)}) copy-start(f32[512,128]{1,0:T(8,128)} %constant.108.clone.into_ref) | copy-start | bytes 786436
  22.6 17.2 %copy-start.8 = (bf16[768,256]{1,0:T(8,128)(2,1)S(1)}, bf16[768,256]{1,0:T(8,128)(2,1)}, u32[]{:S(2)}) copy-start(bf16[768,256]{1,0:T(8,128)(2,1)} %get-tuple-element.42.act_ref) | copy-start | bytes 1179652
  22.6 17.2 %copy-start.24 = (f32[64,32]{1,0:T(8,128)S(1)}, f32[64,32]{1,0:T(8,128)}, u32[]{:S(2)}) copy-start(f32[64,32]{1,0:T(8,128)} %constant.107.clone.split_ref) | copy-start | bytes 24580
  27.4 20.1 %copy-start.30 = (s32[64,128]{1,0:T(8,128)S(1)}, s32[64,128]{1,0:T(8,128)}, u32[]{:S(2)}) copy-start(s32[64,128]{1,0:T(8,128)} %constant.109.clone) | copy-start | bytes 98308
  27.4 20.1 %copy-start.31 = (f32[64,128]{1,0:T(8,128)S(1)}, f32[64,128]{1,0:T(8,128)}, u32[]{:S(2)}) copy-start(f32[64,128]{1,0:T(8,128)} %get-tuple-element.40) | copy-start | bytes 98308
  27.5 18.0 %collective-permute-start.9 = (f32[64,128]{1,0:T(8,128)}, f32[64,128]{1,0:T(8,128)S(1)}, u32[]{:S(2)}, u32[]{:S(2)}) collective-permute-start(f32[64,128]{1,0:T(8,128)} %get-tuple-element.41), channel_id=1, source_target_pairs={{0,1},{1,0},{2,3},{3,2},{4,5},{5,4},{6,7},{7,6},{8,9},{9,8},{10,11... | collective-permute-start | bytes 98312 | tf_op jit(solution)/shard_map/ppermute | solution.py:469
  41.5 66.1 %copy-start.2 = (f32[1,90,4096]{2,0,1:T(1,128)S(1)}, f32[1,90,4096]{2,0,1:T(1,128)}, u32[]{:S(2)}) copy-start(f32[1,90,4096]{2,0,1:T(1,128)} %param.25) | copy-start | bytes 4423684
  41.5 6.0 %collective-permute-start.11 = (f32[64,128]{1,0:T(8,128)S(1)}, f32[64,128]{1,0:T(8,128)S(1)}, u32[]{:S(2)}, u32[]{:S(2)}) collective-permute-start(f32[64,128]{1,0:T(8,128)S(1)} %get-tuple-element.44), channel_id=1, source_target_pairs={{0,2},{1,3},{2,0},{3,1},{4,6},{5,7},{6,4},{7,5},{8,10},{9,11},{10,... | collective-permute-start | bytes 98312 | tf_op jit(solution)/shard_map/ppermute | solution.py:469
  45.4 10.8 %collective-permute-start.5 = (bf16[368,512]{1,0:T(8,128)(2,1)S(1)}, bf16[368,512]{1,0:T(8,128)(2,1)S(1)}, u32[]{:S(2)}, u32[]{:S(2)}) collective-permute-start(bf16[368,512]{1,0:T(8,128)(2,1)S(1)} %fusion.1.refs_0_), channel_id=1, source_target_pairs={{0,4},{4,0},{8,12},{12,8},{16,20},{20,16},{24,28},{28,24},{1,5},{5... | collective-permute-start | bytes 1130504 | tf_op jit(solution)/shard_map/ppermute | solution.py:469
  45.5 12.3 %collective-permute-start.3 = (bf16[368,512]{1,0:T(8,128)(2,1)S(1)}, bf16[368,512]{1,0:T(8,128)(2,1)S(1)}, u32[]{:S(2)}, u32[]{:S(2)}) collective-permute-start(bf16[368,512]{1,0:T(8,128)(2,1)S(1)} %fusion.1.refs_0_), channel_id=1, source_target_pairs={{0,16},{4,20},{8,24},{12,28},{16,0},{20,4},{24,8},{28,12},{1,17},{... | collective-permute-start | bytes 1130504 | tf_op jit(solution)/shard_map/ppermute | solution.py:469
  47.1 34.9 %collective-permute-start.4 = (bf16[368,512]{1,0:T(8,128)(2,1)}, bf16[368,512]{1,0:T(8,128)(2,1)}, u32[]{:S(2)}, u32[]{:S(2)}) collective-permute-start(bf16[368,512]{1,0:T(8,128)(2,1)} %collective-permute-done.2.refs_1_), channel_id=1, source_target_pairs={{0,16},{4,20},{8,24},{12,28},{16,0},{20,4},{24,8},{28,12},{1,17},{... | collective-permute-start | bytes 1130504 | tf_op jit(solution)/shard_map/ppermute | solution.py:469
  47.6 55.4 %copy-start.18 = (bf16[64,128]{1,0:T(8,128)(2,1)}, bf16[64,128]{1,0:T(8,128)(2,1)S(1)}, u32[]{:S(2)}) copy-start(bf16[64,128]{1,0:T(8,128)(2,1)S(1)} %select_convert_fusion.quad_ref) | copy-start | bytes 49156
  47.6 4.7 %collective-permute-start.12 = (bf16[1,64,128]{2,1,0:T(8,128)(2,1)S(1)}, bf16[1,64,128]{2,1,0:T(8,128)(2,1)S(1)}, u32[]{:S(2)}, u32[]{:S(2)}) collective-permute-start(bf16[1,64,128]{2,1,0:T(8,128)(2,1)S(1)} %bitcast.44), channel_id=1, source_target_pairs={{0,2},{1,3},{2,0},{3,1},{4,6},{5,7},{6,4},{7,5},{8,10},{9,11},{10,... | collective-permute-start | bytes 49160 | tf_op jit(solution)/shard_map/ppermute | solution.py:469
  52.3 50.7 %collective-permute-start.24 = (bf16[1920,128]{1,0:T(8,128)(2,1)S(1)}, bf16[1920,128]{1,0:T(8,128)(2,1)S(1)}, u32[]{:S(2)}, u32[]{:S(2)}) collective-permute-start(bf16[1920,128]{1,0:T(8,128)(2,1)S(1)} %get-tuple-element.49), channel_id=1, source_target_pairs={{0,2},{1,3},{2,0},{3,1},{4,6},{5,7},{6,4},{7,5},{8,10},{9,11},{10,... | collective-permute-start | bytes 1474568 | tf_op jit(solution)/shard_map/ppermute | solution.py:469
  54.3 9.5 %collective-permute-start.13 = (bf16[2,64,128]{2,1,0:T(8,128)(2,1)S(1)}, bf16[2,64,128]{2,1,0:T(8,128)(2,1)S(1)}, u32[]{:S(2)}, u32[]{:S(2)}) collective-permute-start(bf16[2,64,128]{2,1,0:T(8,128)(2,1)S(1)} %pad_maximum_fusion.4), channel_id=1, source_target_pairs={{0,1},{1,0},{2,3},{3,2},{4,5},{5,4},{6,7},{7,6},{8,9},{9,8},{10,11... | collective-permute-start | bytes 98312 | tf_op jit(solution)/shard_map/ppermute | solution.py:469
  56.2 0.7 copy-start.10
  56.9 22.9 %collective-permute-start.22 = (bf16[384,128]{1,0:T(8,128)(2,1)S(1)}, bf16[384,128]{1,0:T(8,128)(2,1)S(1)}, u32[]{:S(2)}, u32[]{:S(2)}) collective-permute-start(bf16[384,128]{1,0:T(8,128)(2,1)S(1)} %get-tuple-element.47), channel_id=1, source_target_pairs={{0,2},{1,3},{2,0},{3,1},{4,6},{5,7},{6,4},{7,5},{8,10},{9,11},{10,... | collective-permute-start | bytes 294920 | tf_op jit(solution)/shard_map/ppermute | solution.py:469
  57.8 44.4 %collective-permute-start.6 = (bf16[368,512]{1,0:T(8,128)(2,1)}, bf16[368,512]{1,0:T(8,128)(2,1)S(1)}, u32[]{:S(2)}, u32[]{:S(2)}) collective-permute-start(bf16[368,512]{1,0:T(8,128)(2,1)} %collective-permute-done.2.refs_1_), channel_id=1, source_target_pairs={{0,4},{4,0},{8,12},{12,8},{16,20},{20,16},{24,28},{28,24},{1,5},{5... | collective-permute-start | bytes 1130504 | tf_op jit(solution)/shard_map/ppermute | solution.py:469
  63.7 37.2 %collective-permute-start.7 = (bf16[368,512]{1,0:T(8,128)(2,1)S(1)}, bf16[368,512]{1,0:T(8,128)(2,1)S(1)}, u32[]{:S(2)}, u32[]{:S(2)}) collective-permute-start(bf16[368,512]{1,0:T(8,128)(2,1)S(1)} %collective-permute-done.3.refs_2_), channel_id=1, source_target_pairs={{0,4},{4,0},{8,12},{12,8},{16,20},{20,16},{24,28},{28,24},{1,5},{5... | collective-permute-start | bytes 1130504 | tf_op jit(solution)/shard_map/ppermute | solution.py:469
  63.7 0.8 copy-start.12
  79.8 0.6 copy-start.25
  80.4 4.6 %collective-permute-start.15 = (bf16[4,64,128]{2,1,0:T(8,128)(2,1)}, bf16[4,64,128]{2,1,0:T(8,128)(2,1)}, u32[]{:S(2)}, u32[]{:S(2)}) collective-permute-start(bf16[4,64,128]{2,1,0:T(8,128)(2,1)} %pad_maximum_fusion.3.refs_0_), channel_id=1, source_target_pairs={{0,16},{4,20},{8,24},{12,28},{16,0},{20,4},{24,8},{28,12},{1,17},{... | collective-permute-start | bytes 196616 | tf_op jit(solution)/shard_map/ppermute | solution.py:469
  82.0 35.4 %collective-permute-start.8 = (bf16[368,512]{1,0:T(8,128)(2,1)}, bf16[368,512]{1,0:T(8,128)(2,1)}, u32[]{:S(2)}, u32[]{:S(2)}) collective-permute-start(bf16[368,512]{1,0:T(8,128)(2,1)} %collective-permute-done.4.refs_3_), channel_id=1, source_target_pairs={{0,4},{4,0},{8,12},{12,8},{16,20},{20,16},{24,28},{28,24},{1,5},{5... | collective-permute-start | bytes 1130504 | tf_op jit(solution)/shard_map/ppermute | solution.py:469
  85.0 4.6 %collective-permute-start.14 = (bf16[4,64,128]{2,1,0:T(8,128)(2,1)}, bf16[4,64,128]{2,1,0:T(8,128)(2,1)}, u32[]{:S(2)}, u32[]{:S(2)}) collective-permute-start(bf16[4,64,128]{2,1,0:T(8,128)(2,1)} %pad_maximum_fusion.3.refs_0_), channel_id=1, source_target_pairs={{0,8},{4,12},{8,0},{12,4},{16,24},{20,28},{24,16},{28,20},{1,9},{5... | collective-permute-start | bytes 196616 | tf_op jit(solution)/shard_map/ppermute | solution.py:469
  89.6 6.1 %collective-permute-start.23 = (bf16[576,128]{1,0:T(8,128)(2,1)S(1)}, bf16[576,128]{1,0:T(8,128)(2,1)S(1)}, u32[]{:S(2)}, u32[]{:S(2)}) collective-permute-start(bf16[576,128]{1,0:T(8,128)(2,1)S(1)} %get-tuple-element.48), channel_id=1, source_target_pairs={{0,2},{1,3},{2,0},{3,1},{4,6},{5,7},{6,4},{7,5},{8,10},{9,11},{10,... | collective-permute-start | bytes 442376 | tf_op jit(solution)/shard_map/ppermute | solution.py:469
  95.7 0.7 copy-start.22
  96.3 4.6 %collective-permute-start.19 = (bf16[4,64,128]{2,1,0:T(8,128)(2,1)}, bf16[4,64,128]{2,1,0:T(8,128)(2,1)}, u32[]{:S(2)}, u32[]{:S(2)}) collective-permute-start(bf16[4,64,128]{2,1,0:T(8,128)(2,1)} %collective-permute-done.14.refs_1_), channel_id=1, source_target_pairs={{0,16},{4,20},{8,24},{12,28},{16,0},{20,4},{24,8},{28,12},{1,17},{... | collective-permute-start | bytes 196616 | tf_op jit(solution)/shard_map/ppermute | solution.py:469
  100.9 20.9 %collective-permute-start.16 = (bf16[4,64,128]{2,1,0:T(8,128)(2,1)}, bf16[4,64,128]{2,1,0:T(8,128)(2,1)}, u32[]{:S(2)}, u32[]{:S(2)}) collective-permute-start(bf16[4,64,128]{2,1,0:T(8,128)(2,1)} %pad_maximum_fusion.3.refs_0_), channel_id=1, source_target_pairs={{0,4},{4,0},{8,12},{12,8},{16,20},{20,16},{24,28},{28,24},{1,5},{5... | collective-permute-start | bytes 196616 | tf_op jit(solution)/shard_map/ppermute | solution.py:469
  100.9 0.8 copy-start.16
  101.7 20.1 %collective-permute-start.17 = (bf16[4,64,128]{2,1,0:T(8,128)(2,1)}, bf16[4,64,128]{2,1,0:T(8,128)(2,1)}, u32[]{:S(2)}, u32[]{:S(2)}) collective-permute-start(bf16[4,64,128]{2,1,0:T(8,128)(2,1)} %collective-permute-done.14.refs_1_), channel_id=1, source_target_pairs={{0,4},{4,0},{8,12},{12,8},{16,20},{20,16},{24,28},{28,24},{1,5},{5... | collective-permute-start | bytes 196616 | tf_op jit(solution)/shard_map/ppermute | solution.py:469
  102.2 0.8 copy-start.14
  103.0 18.8 %collective-permute-start.18 = (bf16[4,64,128]{2,1,0:T(8,128)(2,1)}, bf16[4,64,128]{2,1,0:T(8,128)(2,1)}, u32[]{:S(2)}, u32[]{:S(2)}) collective-permute-start(bf16[4,64,128]{2,1,0:T(8,128)(2,1)} %collective-permute-done.15.refs_2_), channel_id=1, source_target_pairs={{0,4},{4,0},{8,12},{12,8},{16,20},{20,16},{24,28},{28,24},{1,5},{5... | collective-permute-start | bytes 196616 | tf_op jit(solution)/shard_map/ppermute | solution.py:469
  103.0 0.8 copy-start.6
  103.8 18.1 %collective-permute-start.20 = (bf16[4,64,128]{2,1,0:T(8,128)(2,1)}, bf16[4,64,128]{2,1,0:T(8,128)(2,1)}, u32[]{:S(2)}, u32[]{:S(2)}) collective-permute-start(bf16[4,64,128]{2,1,0:T(8,128)(2,1)} %collective-permute-done.19.refs_6_), channel_id=1, source_target_pairs={{0,4},{4,0},{8,12},{12,8},{16,20},{20,16},{24,28},{28,24},{1,5},{5... | collective-permute-start | bytes 196616 | tf_op jit(solution)/shard_map/ppermute | solution.py:469
  107.7 1.0 copy-start.9
  108.7 0.7 copy-start.19
  109.4 0.9 copy-start.21
  110.3 0.9 copy-start.23
  111.2 0.9 copy-start.26
  112.1 0.8 copy-start.27
  112.9 0.7 copy-start.28
  113.5 2.5 %copy-start.7 = (bf16[1920,128]{1,0:T(8,128)(2,1)S(1)}, bf16[1920,128]{1,0:T(8,128)(2,1)}, u32[]{:S(2)}) copy-start(bf16[1920,128]{1,0:T(8,128)(2,1)} %copy-done.6) | copy-start | bytes 1474564
  116.0 1.9 %copy-start.1 = (bf16[256,2880]{0,1:T(8,128)(2,1)S(1)}, bf16[256,2880]{0,1:T(8,128)(2,1)}, u32[]{:S(2)}) copy-start(bf16[256,2880]{0,1:T(8,128)(2,1)} %param.23) | copy-start | bytes 4423684
  116.1 2.0 %copy-start.11 = (bf16[368,512]{1,0:T(8,128)(2,1)S(1)}, bf16[368,512]{1,0:T(8,128)(2,1)}, u32[]{:S(2)}) copy-start(bf16[368,512]{1,0:T(8,128)(2,1)} %copy-done.10) | copy-start | bytes 1130500
  116.1 2.1 %copy-start.13 = (bf16[368,512]{1,0:T(8,128)(2,1)S(1)}, bf16[368,512]{1,0:T(8,128)(2,1)}, u32[]{:S(2)}) copy-start(bf16[368,512]{1,0:T(8,128)(2,1)} %copy-done.12) | copy-start | bytes 1130500
  116.1 2.2 %copy-start.15 = (bf16[368,512]{1,0:T(8,128)(2,1)S(1)}, bf16[368,512]{1,0:T(8,128)(2,1)}, u32[]{:S(2)}) copy-start(bf16[368,512]{1,0:T(8,128)(2,1)} %copy-done.14) | copy-start | bytes 1130500
  116.1 2.3 %copy-start.17 = (bf16[368,512]{1,0:T(8,128)(2,1)S(1)}, bf16[368,512]{1,0:T(8,128)(2,1)}, u32[]{:S(2)}) copy-start(bf16[368,512]{1,0:T(8,128)(2,1)} %copy-done.16) | copy-start | bytes 1130500
  118.4 3.5 %copy-start.4 = (bf16[256,1536]{1,0:T(8,128)(2,1)S(1)}, bf16[256,1536]{1,0:T(8,128)(2,1)}, u32[]{:S(2)}) copy-start(bf16[256,1536]{1,0:T(8,128)(2,1)} %lows.1.lows_in) | copy-start | bytes 2359300
  118.4 3.5 %copy-start.20 = (bf16[256,512]{1,0:T(8,128)(2,1)S(1)}, bf16[256,512]{1,0:T(8,128)(2,1)}, u32[]{:S(2)}) copy-start(bf16[256,512]{1,0:T(8,128)(2,1)} %constant.112.clone.across_ref) | copy-start | bytes 786436
